TPU v7x, 32 devices: a whole 2x2x4 slice. The times are simulated.
32 devices in a mesh: dp: 8 (over z, y), mp: 4 (over x, core).
Axes of the slice: x: 2, y: 2, z: 4, core: 2. Of those that a mesh axis runs over, the one named last changes fastest.
Arguments:
- tokens: bfloat16 [32768, 512], P(('dp', 'mp')), may hold values from -6 to 6
- cotangent: bfloat16 [32768, 512], P(('dp', 'mp')), may hold values from -6 to 6
- routes: int32 [32768, 8], P(('dp', 'mp')), may hold values from 0 to 23, all different within a row
- starts: int32 [32768], P(('dp', 'mp')), may hold values from 0 to 3072, as said below
- attn_param: float32 [512, 3226], P(('dp', 'mp'))
- attn_first: float32 [512, 3226], P(('dp', 'mp'))
- attn_second: float32 [512, 3226], P(('dp', 'mp')), as said below
- ffn_param: float32 [2, 512, 2048], P(None, 'dp', 'mp')
- ffn_first: float32 [2, 512, 2048], P(None, 'dp', 'mp')
- ffn_second: float32 [2, 512, 2048], P(None, 'dp', 'mp'), as said below
- rates: float32 [7], replicated, as said below
Outputs:
- layer_out: bfloat16 [32768, 512], P(('dp', 'mp'))
- input_grad: float32 [32768, 512], P(('dp', 'mp'))
- attn_grad: float32 [512, 3226], P(('dp', 'mp'))
- attn_second_new: float32 [512, 3226], P(('dp', 'mp'))
- attn_new: float32 [512, 3226], P(('dp', 'mp'))
- ffn_grad: float32 [2, 512, 2048], P(None, 'dp', 'mp')
- ffn_second_new: float32 [2, 512, 2048], P(None, 'dp', 'mp')
- ffn_new: float32 [2, 512, 2048], P(None, 'dp', 'mp')
- grad_norm: float32 [], replicated
- gain_grad: float32 [512, 2], P(('dp', 'mp'))
Inputs may be any that keep to these rules, and one draw needn't show every extreme that they name: `routes`: each row names 8 different experts. `starts`: sequences are contiguous within each group of 4096 tokens; in half of the groups one sequence fills the group, in the others every sequence has 1024 tokens. `attn_second`: positive. `ffn_second`: positive. `rates`: positive.
All inputs are finite; a program needn't handle non-finite values.
Results may differ from a plain program's by a relative error of at most 0.012.
The roundings to bfloat16 on the way count: a program that leaves them out, or rounds other values in their place, can miss the bound.
Values may be sent and summed in bfloat16 or wider, within the bound.
No kernel may reach another device: no remote copies, remote signals or barrier semaphores. Data moves between devices by JAX's collectives and lax.ppermute only.
A program may use at most 128 MiB of HBM per device.

v0:
```python
import functools
import math

import jax
import jax.numpy as jnp
from jax import lax
from jax.experimental import pallas as pl
from jax.experimental.pallas import tpu as pltpu
from jax.sharding import PartitionSpec as P

HD = 64
E = 24
TOPK = 8
ADAM_STEP = 7
AC = 3226
SPAN = E * HD
PAIRS = E // 2
LANES = 128

NORM_EPS = 1e-05
MASKED = -1e30
CLIP_NORM = 0.1
BETA_FIRST = 0.9
BETA_SECOND = 0.95
ADAM_EPS = 1e-08
WEIGHT_DECAY = 0.1

SCALE = HD ** (-0.5)
LOG2E = math.log2(math.e)
SAFE_SCORE = 40.0
SAFE_VALUE = 1e15
VMEM = 58 << 20

F32 = jnp.float32
BF16 = jnp.bfloat16


def dot(left, right):
    return jnp.dot(left, right, preferred_element_type=F32)


def dot_last(left, right):
    return lax.dot_general(left, right, (((1,), (1,)), ((), ())), preferred_element_type=F32)


def dot_first(left, right):
    return lax.dot_general(left, right, (((0,), (0,)), ((), ())), preferred_element_type=F32)


def turned(values):
    return values.astype(F32).T.astype(values.dtype)


def standardize(values):
    centred = values - jnp.mean(values, -1, keepdims=True)
    factor = lax.rsqrt(jnp.mean(centred * centred, -1, keepdims=True) + NORM_EPS)
    return (centred * factor, factor)


def norm_back(grad_normal, normal, factor):
    return factor * (
        grad_normal
        - jnp.mean(grad_normal, -1, keepdims=True)
        - normal * jnp.mean(grad_normal * normal, -1, keepdims=True)
    )


def lane_index(rows):
    return lax.broadcasted_iota(jnp.int32, (rows, LANES), 1)


def column(values, index, rows):
    return jnp.broadcast_to(values[:, index : index + 1], (rows, LANES))


def pick_pairs(table, chosen):
    picked = jnp.zeros(chosen.shape, table.dtype)
    for pair in range(PAIRS):
        picked = jnp.where(chosen == 2 * pair, table[:, pair * LANES : (pair + 1) * LANES], picked)
    return picked


def place_pairs(parts, chosen):
    columns = []
    for pair in range(PAIRS):
        total = jnp.zeros(chosen[0].shape, parts[0].dtype)
        for part, choice in zip(parts, chosen):
            total = jnp.where(choice == 2 * pair, part, total)
        columns.append(total)
    return jnp.concatenate(columns, 1)


def choices(routes, rows, dtype):
    half = (lane_index(rows) >= HD).astype(jnp.int32)
    return [(column(routes, slot, rows) - half).astype(F32).astype(dtype) for slot in range(TOPK)]


def gains_of(tail):
    return tail.astype(F32).T


def flat_of(index):
    x, y, z = index // 8, index // 4 % 2, index % 4
    return ((z * 2 + y) * 2 + x) * 2


def embed_kernel(x_ref, routes_ref, w_ref, h_ref, kv_ref, gate_ref):
    rows = x_ref.shape[0]
    gain = gains_of(w_ref[:, LANES:])[E : E + 1]
    normal, _ = standardize(x_ref[...].astype(F32))
    h = (normal * gain).astype(BF16)
    h_ref[...] = h
    proj = dot(h, w_ref[...])
    kv_ref[...] = proj[:, :LANES].astype(BF16)
    logits = proj[:, LANES:]
    routes = routes_ref[...]
    lane = lane_index(rows)
    columns = [column(routes, slot, rows) for slot in range(TOPK)]
    chosen = jnp.zeros((rows, LANES), jnp.bool_)
    for route in columns:
        chosen = chosen | (lane == route)
    peak = jnp.max(jnp.where(chosen, logits, MASKED), -1, keepdims=True)
    expo = jnp.where(chosen, jnp.exp(jnp.where(chosen, logits - peak, 0.0)), 0.0)
    dense = expo / jnp.sum(expo, -1, keepdims=True)
    gates = jnp.zeros((rows, LANES), F32)
    for slot, route in enumerate(columns):
        hit = jnp.where(lane == route, dense, 0.0)
        gates = jnp.where(lane == slot, jnp.sum(hit, -1, keepdims=True), gates)
    gate_ref[...] = gates


def embed_call(x, routes, weights, tile=256):
    rows, width = x.shape
    by_row = lambda count: pl.BlockSpec((tile, count), lambda i: (i, 0))
    return pl.pallas_call(
        embed_kernel,
        grid=(rows // tile,),
        in_specs=[by_row(width), by_row(TOPK), pl.BlockSpec(weights.shape, lambda i: (0, 0))],
        out_specs=[by_row(width), by_row(LANES), by_row(LANES)],
        out_shape=[
            jax.ShapeDtypeStruct((rows, width), BF16),
            jax.ShapeDtypeStruct((rows, LANES), BF16),
            jax.ShapeDtypeStruct((rows, LANES), F32),
        ],
        compiler_params=pltpu.CompilerParams(vmem_limit_bytes=VMEM),
        cost_estimate=pl.CostEstimate(
            flops=4 * rows * width * LANES, bytes_accessed=8 * rows * width, transcendentals=0
        ),
        name="embed",
    )(x, routes, weights)


def query_kernel(me_ref, h_ref, routes_ref, near_ref, far_ref, q_ref, w_ref, sems):
    rows = h_ref.shape[0]
    pieces, piece, _ = near_ref.shape

    @pl.when(pl.program_id(0) == 0)
    def _():
        copies = []
        for core, part in enumerate((near_ref, far_ref)):
            for index in range(pieces):
                owner = me_ref[0] ^ (flat_of(index) + core)
                first = pl.multiple_of(owner * piece, piece)
                copies.append(
                    pltpu.make_async_copy(
                        part.at[index], w_ref.at[pl.ds(first, piece), :], sems.at[core * pieces + index]
                    )
                )
        for copy in copies:
            copy.start()
        for copy in copies:
            copy.wait()

    table = dot(h_ref[...], w_ref[...]).astype(BF16)
    for slot, choice in enumerate(choices(routes_ref[...], rows, BF16)):
        q_ref[slot] = pick_pairs(table, choice)


def query_call(me, h, routes, near, far, tile=256):
    rows, width = h.shape
    pieces, piece, cols = near.shape
    by_row = lambda count: pl.BlockSpec((tile, count), lambda i, s: (i, 0))
    return pl.pallas_call(
        query_kernel,
        grid_spec=pltpu.PrefetchScalarGridSpec(
            num_scalar_prefetch=1,
            grid=(rows // tile,),
            in_specs=[
                by_row(width),
                by_row(TOPK),
                pl.BlockSpec(memory_space=pl.ANY),
                pl.BlockSpec(memory_space=pl.ANY),
            ],
            out_specs=[
                pl.BlockSpec((TOPK, tile, LANES), lambda i, s: (0, i, 0)),
                pl.BlockSpec((width, cols), lambda i, s: (0, 0)),
            ],
            scratch_shapes=[pltpu.SemaphoreType.DMA((2 * pieces,))],
        ),
        out_shape=[
            jax.ShapeDtypeStruct((TOPK, rows, LANES), BF16),
            jax.ShapeDtypeStruct((width, cols), BF16),
        ],
        compiler_params=pltpu.CompilerParams(vmem_limit_bytes=VMEM),
        cost_estimate=pl.CostEstimate(
            flops=2 * rows * width * cols, bytes_accessed=8 * rows * width + 2 * width * cols, transcendentals=0
        ),
        name="query",
    )(me, h, routes, near, far)


def spread_keyval(device, kv_refs, key_ref, value_ref):
    devices = len(kv_refs)
    _, block, _ = kv_refs[0].shape
    low_half = lane_index(block) < HD
    for index in range(devices):
        for high in range(2):
            rows = kv_refs[index][high].astype(F32)
            rolled = pltpu.roll(rows, HD, 1)
            span = block_of(device ^ index, high, devices, block)
            key_ref[span, :] = jnp.where(low_half, rows, rolled).astype(BF16)
            value_ref[span, :] = jnp.where(low_half, rolled, rows).astype(BF16)


def block_of(device, high, devices, block):
    place = 2 * devices - 1 - device if high else device
    return pl.ds(pl.multiple_of(place * block, block), block)


def attend_kernel(place_ref, q_ref, *refs):
    *kv_refs, o_ref, log_ref, key_ref, plain_ref, value_ref, acc_ref, peak_ref, bound_ref = refs
    step = pl.program_id(0)
    slots, tile, _ = q_ref.shape
    rows = slots * tile
    width = 512

    @pl.when(step == 0)
    def _():
        spread_keyval(place_ref[2, 0], kv_refs, key_ref, plain_ref)
        value_ref[:, :LANES] = plain_ref[...]
        value_ref[:, LANES:] = jnp.ones((value_ref.shape[0], LANES), BF16)
        keys = key_ref[...].astype(F32)
        bound_ref[0] = jnp.max(jnp.sum(keys * keys, -1, keepdims=True)) * 0.5
        bound_ref[1] = jnp.max(jnp.abs(plain_ref[...].astype(F32)))

    here = place_ref[0, step]
    lower = pl.multiple_of(place_ref[1, step], width)
    q = q_ref[...].reshape(rows, LANES)
    qf = q.astype(F32)
    longest = jnp.max(jnp.sum(qf * qf, -1, keepdims=True))
    plain = (longest * bound_ref[0] <= (SAFE_SCORE / SCALE) ** 2) & (bound_ref[1] <= SAFE_VALUE)
    full = (here - lower) // width
    last = pl.multiple_of(lower + full * width, width)
    token = lax.broadcasted_iota(jnp.int32, (tile, width), 0) + here
    allowed = (lax.broadcasted_iota(jnp.int32, (tile, width), 1) + last) <= token
    allowed = jnp.broadcast_to(allowed[None], (slots, tile, width)).reshape(rows, width)

    def finish(out, logs):
        o_ref[...] = out.reshape(slots, tile, LANES)
        logs = logs.reshape(slots, tile, LANES)
        lane = lane_index(tile)
        packed = jnp.zeros((tile, LANES), F32)
        for slot in range(slots):
            packed = jnp.where(lane == slot, logs[slot], packed)
        log_ref[...] = packed

    pairs = full // 2

    @pl.when(plain)
    def _():
        for count in (1, 2):

            @pl.when(full % 2 == count - 1)
            def _(count=count):
                span = pl.ds(pl.multiple_of(lower + pairs * 2 * width, width), count * width)
                expo = jnp.exp2(dot_last(q, key_ref[span, :]) * (SCALE * LOG2E))
                edge = jnp.where(allowed, expo[:, (count - 1) * width :], 0.0).astype(BF16)
                expo = jnp.concatenate([expo[:, :width].astype(BF16), edge], 1) if count > 1 else edge
                acc_ref[...] = dot(expo, value_ref[span, :])

        def body(index, carry):
            span = pl.ds(pl.multiple_of(lower + index * 2 * width, width), 2 * width)
            expo = jnp.exp2(dot_last(q, key_ref[span, :]) * (SCALE * LOG2E)).astype(BF16)
            acc_ref[...] += dot(expo, value_ref[span, :])
            return carry

        lax.fori_loop(0, pairs, body, 0)
        total = acc_ref[:, LANES:]
        finish(acc_ref[:, :LANES] / total, jnp.log2(total))

    @pl.when(jnp.logical_not(plain))
    def _():
        def scaled(span):
            return dot_last(q, key_ref[span, :]) * (SCALE * LOG2E)

        scores = jnp.where(allowed, scaled(pl.ds(last, width)), MASKED)
        peak = jnp.max(scores, -1, keepdims=True)
        peak_ref[...] = jnp.broadcast_to(peak, (rows, LANES))
        acc_ref[...] = dot(jnp.exp2(scores - peak).astype(BF16), value_ref[pl.ds(last, width), :])

        def body(index, carry):
            span = pl.ds(pl.multiple_of(lower + index * width, width), width)
            scores = scaled(span)
            before = peak_ref[:, :1]
            peak = jnp.maximum(before, jnp.max(scores, -1, keepdims=True))
            peak_ref[...] = jnp.broadcast_to(peak, (rows, LANES))
            expo = jnp.exp2(scores - peak).astype(BF16)
            acc_ref[...] = acc_ref[...] * jnp.exp2(before - peak) + dot(expo, value_ref[span, :])
            return carry

        lax.fori_loop(0, full, body, 0)
        total = acc_ref[:, LANES:]
        finish(acc_ref[:, :LANES] / total, peak_ref[...] + jnp.log2(total))


def attend_call(place, q, kv, tile=128):
    slots, rows, _ = q.shape
    count = len(kv) * kv[0].shape[0] * kv[0].shape[1]
    return pl.pallas_call(
        attend_kernel,
        grid_spec=pltpu.PrefetchScalarGridSpec(
            num_scalar_prefetch=1,
            grid=(rows // tile,),
            in_specs=[
                pl.BlockSpec((slots, tile, LANES), lambda i, s: (0, i, 0)),
                *[pl.BlockSpec(part.shape, lambda i, s: (0, 0, 0)) for part in kv],
            ],
            out_specs=[
                pl.BlockSpec((slots, tile, LANES), lambda i, s: (0, i, 0)),
                pl.BlockSpec((tile, LANES), lambda i, s: (i, 0)),
                pl.BlockSpec((count, LANES), lambda i, s: (0, 0)),
                pl.BlockSpec((count, LANES), lambda i, s: (0, 0)),
            ],
            scratch_shapes=[
                pltpu.VMEM((count, 2 * LANES), BF16),
                pltpu.VMEM((slots * tile, 2 * LANES), F32),
                pltpu.VMEM((slots * tile, LANES), F32),
                pltpu.SMEM((2,), F32),
            ],
        ),
        out_shape=[
            jax.ShapeDtypeStruct((slots, rows, LANES), F32),
            jax.ShapeDtypeStruct((rows, LANES), F32),
            jax.ShapeDtypeStruct((count, LANES), BF16),
            jax.ShapeDtypeStruct((count, LANES), BF16),
        ],
        compiler_params=pltpu.CompilerParams(vmem_limit_bytes=VMEM),
        cost_estimate=pl.CostEstimate(
            flops=8 * slots * rows * count * LANES, bytes_accessed=8 * slots * rows * LANES, transcendentals=0
        ),
        name="attend",
    )(place, q, *kv)


def attend_back_kernel(piece, pieces, groups, *refs):
    first, final = piece == 0, piece == pieces - 1
    refs = list(refs)
    take = lambda count: [refs.pop(0) for _ in range(count)]
    place_ref, q_ref, do_ref, log_ref, delta_ref, routes_ref, key_ref, value_ref = take(8)
    if not first:
        (sums_in,) = take(1)
    if final:
        (h_ref,) = take(1)
        before_refs = take(pieces - 1)
    (all_ref,) = take(1)
    outs = take(4 if final else 1)
    dq_ref, dkey_ref, dvalue_ref, sems = take(4)
    step = pl.program_id(0)
    steps = pl.num_programs(0)
    slots, tile, _ = q_ref.shape
    rows = slots * tile
    width = 512

    @pl.when(step == 0)
    def _():
        dkey_ref[...] = jnp.zeros_like(dkey_ref)
        dvalue_ref[...] = jnp.zeros_like(dvalue_ref)
        if not first:
            copies = [
                pltpu.make_async_copy(sums_in.at[0], dkey_ref.at[pl.ds(0, HD), :], sems.at[0]),
                pltpu.make_async_copy(sums_in.at[1], dvalue_ref.at[pl.ds(0, HD), :], sems.at[1]),
            ]
            for copy in copies:
                copy.start()
            for copy in copies:
                copy.wait()

    here = place_ref[0, piece + pieces * step]
    lower = place_ref[1, piece + pieces * step]
    q = q_ref[...].reshape(rows, LANES)
    do = do_ref[...].reshape(rows, LANES)
    q_turned = turned(q)
    do_turned = turned(do)
    logs = log_ref[...]
    deltas = delta_ref[...]
    logs = jnp.concatenate([column(logs, slot, tile) for slot in range(slots)], 0)
    deltas = jnp.concatenate([column(deltas, slot, tile) for slot in range(slots)], 0)
    full = (here - lower) // width
    last = pl.multiple_of(lower + full * width, width)
    token = lax.broadcasted_iota(jnp.int32, (tile, width), 0) + here
    allowed = (lax.broadcasted_iota(jnp.int32, (tile, width), 1) + last) <= token
    allowed = jnp.broadcast_to(allowed[None], (slots, tile, width)).reshape(rows, width)

    def wide(values):
        return jnp.concatenate([values] * (width // LANES), 1)

    def one(start, masked):
        span = pl.ds(start, width)
        keys = key_ref[span, :]
        scores = dot_last(q, keys)
        probs = jnp.exp2(scores * (SCALE * LOG2E) - wide(logs))
        if masked:
            probs = jnp.where(allowed, probs, 0.0)
        dprobs = dot_last(do, value_ref[span, :])
        dscores = (probs * (dprobs - wide(deltas))).astype(BF16)
        dvalue_ref[:, span] += dot(do_turned, probs.astype(BF16))
        dkey_ref[:, span] += dot(q_turned, dscores)
        return dot(dscores, keys)

    dq_ref[...] = one(last, True)

    def body(index, carry):
        dq_ref[...] += one(pl.multiple_of(lower + index * width, width), False)
        return carry

    lax.fori_loop(0, full, body, 0)

    dq = (dq_ref[...] * SCALE).astype(BF16).reshape(slots, tile, LANES)
    mine = pl.ds(pl.multiple_of(step * tile, tile), tile)
    all_ref[mine, :] = place_pairs([dq[slot] for slot in range(slots)], choices(routes_ref[...], tile, BF16))

    @pl.when(step == steps - 1)
    def _():
        if not final:
            dkey_ref[:HD] += dkey_ref[HD:]
            dvalue_ref[:HD] += dvalue_ref[HD:]
            copies = [
                pltpu.make_async_copy(dkey_ref.at[pl.ds(0, HD), :], outs[0].at[0], sems.at[0]),
                pltpu.make_async_copy(dvalue_ref.at[pl.ds(0, HD), :], outs[0].at[1], sems.at[1]),
            ]
            for copy in copies:
                copy.start()
            for copy in copies:
                copy.wait()
            return
        kv_keep, kv_send, gq_keep, gq_send = outs
        _, _, block, _ = kv_keep.shape
        device = place_ref[2, 0]
        for index in range(4):
            target = kv_send if index % 2 else kv_keep
            for high in range(2):
                span = block_of(device ^ index, high, 4, block)
                dkeys = (dkey_ref[:HD, span] + dkey_ref[HD:, span]) * SCALE
                dvalues = dvalue_ref[:HD, span] + dvalue_ref[HD:, span]
                target[index // 2, high] = jnp.concatenate([dkeys, dvalues], 0).T.astype(BF16)
        gq = dot(turned(h_ref[...]), in_rows([*before_refs, all_ref], tile))
        if groups == 8:
            scatter_rows(gq, gq_keep, gq_send, device % 2)
        else:
            gq_keep[...] = gq.astype(BF16)
            gq_send[...] = jnp.zeros_like(gq_send)


def in_rows(parts, tile):
    return jnp.concatenate([part[:tile] for part in parts] + [part[tile:] for part in parts], 0)


def scatter_rows(grad, keep, send, core):
    for x in range(2):
        for y in range(2):
            for z in range(4):
                base = (((z * 2 + y) * 2 + x) * 2) * 16
                low = grad[base : base + 16].astype(BF16)
                high = grad[base + 16 : base + 32].astype(BF16)
                keep[y, z, x] = jnp.where(core == 0, low, high)
                send[y, z, x] = jnp.where(core == 0, high, low)


def attend_back_call(piece, pieces, groups, where, q, do, logs, deltas, routes, keys, values, carried, h, before):
    slots, rows, _ = q.shape
    count = keys.shape[0]
    width = h.shape[1]
    tile = rows // (2 * pieces)
    final = piece == pieces - 1
    whole = lambda shape: pl.BlockSpec(shape, lambda i, s: (0,) * len(shape))
    anywhere = pl.BlockSpec(memory_space=pl.ANY)
    by_slot = pl.BlockSpec((slots, tile, LANES), lambda i, s: (0, piece + pieces * i, 0))
    by_row = lambda cols: pl.BlockSpec((tile, cols), lambda i, s: (piece + pieces * i, 0))
    in_specs = [
        by_slot, by_slot, by_row(LANES), by_row(LANES), by_row(TOPK), whole(keys.shape), whole(values.shape),
    ]
    in_specs += [anywhere] * len(carried)
    extra = [h, *before] if final else []
    in_specs += [whole(array.shape) for array in extra]
    out_specs = [whole((2 * tile, SPAN))]
    out_shape = [jax.ShapeDtypeStruct((2 * tile, SPAN), BF16)]
    if final:
        kv_shape = (2, 2, rows // 2, LANES)
        gq_shape = (2, 4, 2, 16, SPAN) if groups == 8 else (width, SPAN)
        off_shape = gq_shape if groups == 8 else (8, LANES)
        for shape in (kv_shape, kv_shape, gq_shape, off_shape):
            out_specs.append(whole(shape))
            out_shape.append(jax.ShapeDtypeStruct(shape, BF16))
    else:
        out_specs.append(anywhere)
        out_shape.append(jax.ShapeDtypeStruct((2, HD, count), F32))
    return pl.pallas_call(
        functools.partial(attend_back_kernel, piece, pieces, groups),
        grid_spec=pltpu.PrefetchScalarGridSpec(
            num_scalar_prefetch=1,
            grid=(2,),
            in_specs=in_specs,
            out_specs=out_specs,
            scratch_shapes=[
                pltpu.VMEM((slots * tile, LANES), F32),
                pltpu.VMEM((LANES, count), F32),
                pltpu.VMEM((LANES, count), F32),
                pltpu.SemaphoreType.DMA((2,)),
            ],
        ),
        out_shape=out_shape,
        compiler_params=pltpu.CompilerParams(vmem_limit_bytes=VMEM),
        cost_estimate=pl.CostEstimate(
            flops=10 * slots * 2 * tile * count * LANES, bytes_accessed=16 * slots * tile * LANES, transcendentals=0
        ),
        name="attend_back",
    )(where, q, do, logs, deltas, routes, keys, values, *carried, *extra)


def query_back_kernel(dlog_ref, wq_ref, wr_ref, *refs):
    *all_refs, dh_ref = refs
    rows = in_rows(all_refs, all_refs[0].shape[0] // 2)
    dh_ref[...] = dot_last(rows, wq_ref[...]) + dot_last(dlog_ref[...], wr_ref[...])


def query_back_call(dlogits, wq, wk, parts):
    rows = dlogits.shape[0]
    width = wq.shape[0]
    cols = lambda size, index: pl.BlockSpec((width, size), lambda i: (0, index))
    whole = lambda shape: pl.BlockSpec(shape, lambda i: (0,) * len(shape))
    return pl.pallas_call(
        query_back_kernel,
        grid=(1,),
        in_specs=[
            whole(dlogits.shape), cols(SPAN, 0), cols(LANES, 1), *[whole(part.shape) for part in parts],
        ],
        out_specs=whole((rows, width)),
        out_shape=jax.ShapeDtypeStruct((rows, width), F32),
        compiler_params=pltpu.CompilerParams(vmem_limit_bytes=VMEM),
        cost_estimate=pl.CostEstimate(
            flops=2 * rows * width * (SPAN + LANES), bytes_accessed=4 * rows * (SPAN + width), transcendentals=0
        ),
        name="query_back",
    )(dlogits, wq, wk, *parts)


def middle_kernel(groups, *refs):
    refs = list(refs)
    take = lambda count: [refs.pop(0) for _ in range(count)]
    core_ref, x_hbm, dy_hbm, o_hbm, gate_ref, routes_ref, tail_ref = take(7)
    weights_in = take(8 if groups == 8 else 3)
    out_hbm, dmid_hbm, do_hbm, delta_ref, dlog_ref, gain_ref = take(6)
    outs_hbm = take(4 if groups == 8 else 3)
    x_ref, dy_ref, o_ref, comb_ref, mid_ref, normal_ref, acc_ref, dh_ref, dcomb_ref, out_ref, do_ref = take(11)
    wo_in, w1_in, w2_in = take(3)
    in_sems, out_sems = take(2)
    outs = refs
    rows, width = x_ref.shape
    part = 256
    cols = 512
    count = [0]

    def copy(source, target):
        count[0] += 1
        return pltpu.make_async_copy(source, target, in_sems.at[count[0] - 1])

    slot_copies = [copy(o_hbm.at[slot], o_ref.at[slot]) for slot in range(TOPK)]
    x_copy, dy_copy = copy(x_hbm, x_ref), copy(dy_hbm, dy_ref)
    if groups == 8:
        flat = core_ref[0]
        my_x, my_y, core = flat // 2 % 2, flat // 4 % 2, flat % 2
        wo_copies, w1_copies, w2_copies = [], [], []
        for index in range(8):
            other_core, other = index // 4, index % 4
            for y_turn in range(2):
                y = my_y ^ y_turn
                part_a = weights_in[4 * other_core + (other // 2)]
                x = my_x ^ (other // 2)
                mp = 2 * x + (core ^ other_core)
                across = pl.ds(pl.multiple_of(mp * cols, cols), cols)
                if other % 2 == 0:
                    wo_copies.append(copy(part_a.at[y_turn, :, 4:6], wo_in.at[:, y, mp, 0:2]))
                    w1_copies.append(copy(part_a.at[y_turn, :, 0:4], w1_in.at[:, y, :, :, across]))
                else:
                    part_b = weights_in[4 * other_core + 2 + y_turn]
                    x_turn = other // 2
                    wo_copies.append(copy(part_b.at[x_turn, :, 4:5], wo_in.at[:, y, mp, 2:3]))
                    w2_copies.append(copy(part_b.at[x_turn, :, 0:4], w2_in.at[:, y, :, :, across]))
    else:
        wo_copies, w1_copies, w2_copies = [
            [copy(source, target)] for source, target in zip(weights_in, (wo_in, w1_in, w2_in))
        ]
    for one in (*slot_copies, *wo_copies, x_copy, *w1_copies, dy_copy, *w2_copies):
        one.start()
    view = lambda ref: ref[...].reshape(width, -1)
    third = lambda ref, index: ref[:, :, :, index].reshape(width, cols)

    gain = gains_of(tail_ref[...])[E + 1 : E + 2]
    for one in slot_copies:
        one.wait()

    def combine(index, carry):
        mine = pl.ds(pl.multiple_of(index * part, part), part)
        gates = gate_ref[mine, :]
        weighted = [(column(gates, slot, part) * o_ref[slot, mine, :]).astype(BF16) for slot in range(TOPK)]
        comb_ref[mine, :] = place_pairs(weighted, choices(routes_ref[mine, :], part, BF16))
        return carry

    lax.fori_loop(0, rows // part, combine, 0)
    for one in (*wo_copies, x_copy):
        one.wait()
    mid = x_ref[...].astype(F32)
    if groups == 8:
        for index in range(3):
            mid = mid + dot_last(comb_ref[:, index * cols : (index + 1) * cols], third(wo_in, index))
    else:
        mid = mid + dot_last(comb_ref[...], wo_in[...])
    mid_ref[...] = mid
    normal, factor = standardize(mid)
    normal_ref[...] = normal
    h2 = (normal * gain).astype(BF16)
    for one in (*w1_copies, dy_copy, *w2_copies):
        one.wait()
    dy = dy_ref[...]
    w1, w2 = view(w1_in), view(w2_in)

    for index in range(w1.shape[1] // cols):
        span = slice(index * cols, (index + 1) * cols)
        up, down = w1[:, span], w2[:, span]
        pre = dot(h2, up)
        dact = dot(dy, down)
        sigma = jax.nn.sigmoid(pre)
        act = (pre * sigma).astype(BF16)
        dpre = (dact * (sigma * (1.0 + pre * (1.0 - sigma)))).astype(BF16)
        branch = dot_last(act, down)
        dh2 = dot_last(dpre, up)
        if index == 0:
            acc_ref[...] = branch
            dh_ref[...] = dh2
        else:
            acc_ref[...] += branch
            dh_ref[...] += dh2
        g1 = dot_first(h2, dpre).astype(BF16)
        g2 = dot_first(dy, act).astype(BF16)
        if groups != 8:
            outs[0][:, span] = g1
            outs[1][:, span] = g2
            continue
        for mine, (a, b) in ((True, (outs[0], outs[2])), (False, (outs[1], outs[3]))):

            @pl.when((core_ref[0] % 2 == index % 2) == mine)
            def _(a=a, b=b, g1=g1, g2=g2, x=index // 2):
                for owner in range(8):
                    piece = slice(owner * 64, owner * 64 + 64)
                    a[x, owner % 2, owner // 2, :64] = g1[piece]
                    b[owner % 2, x, owner // 2, :64] = g2[piece]

    out_ref[...] = (mid_ref[...] + acc_ref[...]).astype(BF16)
    out_copy = pltpu.make_async_copy(out_ref, out_hbm, out_sems.at[0])
    out_copy.start()
    dh2 = dh_ref[...]
    normal = normal_ref[...]
    gain_ref[...] = jnp.sum(dh2 * normal, 0, keepdims=True)
    dmid = dy.astype(F32) + norm_back(dh2 * gain, normal, factor)
    mid_ref[...] = dmid
    dmid_copy = pltpu.make_async_copy(mid_ref, dmid_hbm, out_sems.at[1])
    dmid_copy.start()
    dmid_b = dmid.astype(BF16)
    if groups == 8:
        for index in range(3):
            span = slice(index * cols, (index + 1) * cols)
            dcomb_ref[:, span] = dot(dmid_b, third(wo_in, index)).astype(BF16)
    else:
        dcomb_ref[...] = dot(dmid_b, wo_in[...]).astype(BF16)
    go = dot_first(dmid_b, comb_ref[...]).astype(BF16)
    if groups == 8:
        for core in range(2):

            @pl.when(core_ref[0] % 2 == core)
            def _(pairs=((outs[0], outs[2]), (outs[1], outs[3])), core=core):
                for owner in range(32):
                    z, y, x, c = owner // 8, owner // 4 % 2, owner // 2 % 2, owner % 2
                    a, b = pairs[c ^ core]
                    mine = slice(owner * 16, owner * 16 + 16)
                    a[x, y, z, 64:80] = go[mine, :512]
                    a[x, y, z, 80:] = go[mine, 512:1024]
                    b[y, x, z, 64:] = go[mine, 1024:]
    else:
        outs[2][...] = go

    grad_copies = [
        pltpu.make_async_copy(source, target, out_sems.at[3 + index])
        for index, (source, target) in enumerate(zip(outs, outs_hbm))
    ]
    for one in grad_copies:
        one.start()

    def spread(index, carry):
        mine = pl.ds(pl.multiple_of(index * part, part), part)
        gates = gate_ref[mine, :]
        routes = routes_ref[mine, :]
        lane = lane_index(part)
        dcomb = dcomb_ref[mine, :]
        gate_grads = jnp.zeros((part, LANES), F32)
        for slot, choice in enumerate(choices(routes, part, BF16)):
            picked = pick_pairs(dcomb, choice).astype(F32)
            do_ref[slot, mine, :] = (column(gates, slot, part) * picked).astype(BF16)
            total = jnp.sum(o_ref[slot, mine, :] * picked, -1, keepdims=True)
            gate_grads = jnp.where(lane == slot, total, gate_grads)
        weighted = gates * gate_grads
        delta_ref[mine, :] = weighted
        dsel = weighted - gates * jnp.sum(weighted, -1, keepdims=True)
        dlogits = jnp.zeros((part, LANES), F32)
        for slot in range(TOPK):
            dlogits = jnp.where(lane == column(routes, slot, part), column(dsel, slot, part), dlogits)
        dlog_ref[mine, :] = dlogits.astype(BF16)
        return carry

    lax.fori_loop(0, rows // part, spread, 0)
    do_copy = pltpu.make_async_copy(do_ref, do_hbm, out_sems.at[2])
    do_copy.start()
    for one in (out_copy, dmid_copy, do_copy, *grad_copies):
        one.wait()


def middle_call(groups, core, x, dy, o, gates, routes, front, weights):
    rows, width = x.shape
    hidden = 2048
    whole = lambda shape: pl.BlockSpec(shape, lambda i, s: (0,) * len(shape))
    anywhere = pl.BlockSpec(memory_space=pl.ANY)
    if groups == 8:
        grads = [(2, 2, 4, 96, 512), (2, 2, 4, 96, 512), (2, 2, 4, 80, 512), (2, 2, 4, 80, 512)]
        held = [(4, 2, 4, 3, 16, 512), (4, 2, 4, 16, hidden), (4, 2, 4, 16, hidden)]
    else:
        grads = [(width, hidden), (width, hidden), (width, SPAN)]
        held = [(width, SPAN), (width, hidden), (width, hidden)]
    return pl.pallas_call(
        functools.partial(middle_kernel, groups),
        grid_spec=pltpu.PrefetchScalarGridSpec(
            num_scalar_prefetch=1,
            grid=(1,),
            in_specs=[
                anywhere, anywhere, anywhere, whole(gates.shape), whole(routes.shape),
                pl.BlockSpec((width, LANES), lambda i, s: (0, 1)), *[anywhere] * len(weights),
            ],
            out_specs=[
                anywhere, anywhere, anywhere, whole((rows, LANES)), whole((rows, LANES)), whole((1, width)),
                *[anywhere] * len(grads),
            ],
            scratch_shapes=[
                pltpu.VMEM((rows, width), BF16),
                pltpu.VMEM((rows, width), BF16),
                pltpu.VMEM((TOPK, rows, LANES), F32),
                pltpu.VMEM((rows, SPAN), BF16),
                pltpu.VMEM((rows, width), F32),
                pltpu.VMEM((rows, width), F32),
                pltpu.VMEM((rows, width), F32),
                pltpu.VMEM((rows, width), F32),
                pltpu.VMEM((rows, SPAN), BF16),
                pltpu.VMEM((rows, width), BF16),
                pltpu.VMEM((TOPK, rows, LANES), BF16),
                *[pltpu.VMEM(shape, BF16) for shape in held],
                pltpu.SemaphoreType.DMA((42,)),
                pltpu.SemaphoreType.DMA((7,)),
                *[pltpu.VMEM(shape, BF16) for shape in grads],
            ],
        ),
        out_shape=[
            jax.ShapeDtypeStruct((rows, width), BF16),
            jax.ShapeDtypeStruct((rows, width), F32),
            jax.ShapeDtypeStruct((TOPK, rows, LANES), BF16),
            jax.ShapeDtypeStruct((rows, LANES), F32),
            jax.ShapeDtypeStruct((rows, LANES), BF16),
            jax.ShapeDtypeStruct((1, width), F32),
            *[jax.ShapeDtypeStruct(shape, BF16) for shape in grads],
        ],
        compiler_params=pltpu.CompilerParams(vmem_limit_bytes=VMEM),
        cost_estimate=pl.CostEstimate(
            flops=2 * rows * width * (6 * hidden + 3 * SPAN), bytes_accessed=16 * rows * width, transcendentals=0
        ),
        name="middle",
    )(core, x, dy, o, gates, routes, front, *weights)


def post_kernel(x_ref, h_ref, dmid_ref, dh_ref, keep_ref, recv_ref, dlog_ref, gain2_ref, w_ref, grad_ref, gk_ref, sum_ref):
    step = pl.program_id(0)
    gain = gains_of(w_ref[:, LANES:])[E : E + 1]
    normal, factor = standardize(x_ref[...].astype(F32))
    dkv = (keep_ref[...].astype(F32) + recv_ref[...].astype(F32)).astype(BF16)
    dh = dh_ref[...] + dot_last(dkv, w_ref[:, :LANES])
    grad_ref[...] = (dmid_ref[...] + norm_back(dh * gain, normal, factor)).astype(grad_ref.dtype)
    gain1 = jnp.sum(dh * normal, 0, keepdims=True)
    width = gain1.shape[1]
    row = lax.broadcasted_iota(jnp.int32, (LANES, width), 0)
    gain2 = jnp.where(step == 0, gain2_ref[...], 0.0)
    gains = jnp.where(row == E, gain1, jnp.where(row == E + 1, gain2, 0.0))
    h_turned = turned(h_ref[...])
    keyval = dot(h_turned, dkv)
    router = dot(h_turned, dlog_ref[...]) + gains.T

    @pl.when(step == 0)
    def _():
        sum_ref[:, :LANES] = keyval
        sum_ref[:, LANES:] = router

    @pl.when(step > 0)
    def _():
        sum_ref[:, :LANES] += keyval
        sum_ref[:, LANES:] += router

    @pl.when(step == pl.num_programs(0) - 1)
    def _():
        gk_ref[...] = sum_ref[...].astype(BF16)


def post_call(x, h, dmid, dh, keep, recv, dlogits, gain2, weights, tile=256):
    rows, width = x.shape
    by_row = lambda cols: pl.BlockSpec((tile, cols), lambda i: (i, 0))
    return pl.pallas_call(
        post_kernel,
        grid=(rows // tile,),
        in_specs=[
            by_row(width), by_row(width), by_row(width), by_row(width), by_row(LANES), by_row(LANES), by_row(LANES),
            pl.BlockSpec((1, width), lambda i: (0, 0)),
            pl.BlockSpec((width, 2 * LANES), lambda i: (0, 0)),
        ],
        out_specs=[by_row(width), pl.BlockSpec((width, 2 * LANES), lambda i: (0, 0))],
        out_shape=[
            jax.ShapeDtypeStruct((rows, width), BF16),
            jax.ShapeDtypeStruct((width, 2 * LANES), BF16),
        ],
        scratch_shapes=[pltpu.VMEM((width, 2 * LANES), F32)],
        compiler_params=pltpu.CompilerParams(vmem_limit_bytes=VMEM),
        cost_estimate=pl.CostEstimate(
            flops=6 * rows * width * LANES, bytes_accessed=16 * rows * width, transcendentals=0
        ),
        name="finish",
    )(x, h, dmid, dh, keep, recv, dlogits, gain2, weights)


RING = ((0, 1), (1, 2), (2, 3), (3, 0))
SWAP = ((1, 3), (3, 1))


def halves(rows, place):
    half = rows.shape[0] // 2
    outer = (place == 0) | (place == 3)
    first = lax.dynamic_slice_in_dim(rows, jnp.where(outer, half, 0), half, 0)
    second = lax.dynamic_slice_in_dim(rows, jnp.where(place == 1, half, 0), half, 0)
    return first, second


def deal(rows, sent, place):
    half = rows.shape[0] // 2
    ring = lax.ppermute(sent[0], "mp", RING)
    swap = lax.ppermute(sent[1], "mp", SWAP)
    low = jnp.where(place == 0, rows[:half], jnp.where(place == 3, swap, ring))
    high = jnp.where(place == 2, rows[half:], jnp.where(place == 1, swap, ring))
    return jnp.concatenate([low, high], 0)


def gather_back(rows, place):
    half = rows.shape[0] // 2
    first, second = halves(rows, place)
    ring = lax.ppermute(first, "mp", tuple((b, a) for a, b in RING))
    swap = lax.ppermute(second, "mp", SWAP)
    top = jnp.where(place == 0, rows[:half], jnp.where(place == 3, swap, ring))
    bottom = jnp.where(place == 2, rows[half:], jnp.where(place == 1, swap, ring))
    return jnp.concatenate([top, bottom], 0)


OTHER_CORE = ((0, 1), (1, 0), (2, 3), (3, 2))
OTHER_X = ((0, 2), (2, 0), (1, 3), (3, 1))


def swap_core(values):
    return lax.ppermute(values, "mp", OTHER_CORE)


def swap_x(values):
    return lax.ppermute(values, "mp", OTHER_X)


def swap_y(values):
    return lax.ppermute(values, "dp", tuple((i, i ^ 1) for i in range(8)))


def swap_z(values, turn):
    return lax.ppermute(values, "dp", tuple((i, i ^ (2 * turn)) for i in range(8)))


def at(values, index):
    return lax.dynamic_index_in_dim(values, index, 0, keepdims=False)


def added(left, right):
    return (left.astype(F32) + right.astype(F32)).astype(BF16)


def gather_z(shard, my_z):
    turns = [shard] + [swap_z(shard, turn) for turn in (1, 2, 3)]
    rows = []
    for z in range(4):
        row = turns[3]
        for turn in (2, 1, 0):
            row = jnp.where(my_z == z ^ turn, turns[turn], row)
        rows.append(row)
    return jnp.stack(rows)


def after(values, others):
    return lax.optimization_barrier((values, others))[0]


def tied(first, second):
    return lax.optimization_barrier((first, second))


def adam_step(param, first, second, grad, rate, decay):
    first_new = BETA_FIRST * first + (1.0 - BETA_FIRST) * grad
    second_new = BETA_SECOND * second + (1.0 - BETA_SECOND) * grad * grad
    first_hat = first_new / (1.0 - BETA_FIRST**ADAM_STEP)
    second_hat = second_new / (1.0 - BETA_SECOND**ADAM_STEP)
    param_new = param - rate * (first_hat / (jnp.sqrt(second_hat) + ADAM_EPS) + decay * param)
    return (second_new, param_new)


def update_kernel(
    rates_ref, squares_ref, gq_ref, go_ref, gk_ref, ffn_ref,
    ap_ref, am_ref, av_ref, fp_ref, fm_ref, fv_ref,
    ag_ref, avn_ref, apn_ref, fg_ref, fvn_ref, fpn_ref, norm_ref, gain_ref,
):
    norm = jnp.sqrt(jnp.sum(squares_ref[...], 0)[:1, :1])
    norm_ref[...] = norm
    factor = jnp.minimum(1.0, CLIP_NORM / norm)
    tail = AC - 2 * SPAN
    for source, span, rate in (
        (gq_ref, slice(0, SPAN), rates_ref[0]),
        (go_ref, slice(SPAN, 2 * SPAN), rates_ref[1]),
        (gk_ref, slice(2 * SPAN, AC), None),
    ):
        decay = WEIGHT_DECAY
        grad = source[...] * factor
        if rate is None:
            grad = grad[:, :tail]
            place = lax.broadcasted_iota(jnp.int32, (1, tail), 1)
            rate = jnp.where(
                place < 2 * HD, rates_ref[2], jnp.where(place < 2 * HD + E, rates_ref[3], rates_ref[4])
            )
            decay = jnp.where(place < 2 * HD + E, WEIGHT_DECAY, 0.0)
            gain_ref[...] = grad[:, tail - 2 :]
        ag_ref[:, span] = grad
        avn_ref[:, span], apn_ref[:, span] = adam_step(
            ap_ref[:, span], am_ref[:, span], av_ref[:, span], grad, rate, decay
        )
    for index in range(2):
        grad = ffn_ref[index] * factor
        fg_ref[index] = grad
        fvn_ref[index], fpn_ref[index] = adam_step(
            fp_ref[index], fm_ref[index], fv_ref[index], grad, rates_ref[5 + index], WEIGHT_DECAY
        )


def update_call(rates, squares, gq, go, gk, ffn, attn, ffn_state):
    rows = gq.shape[0]
    attn_shape = jax.ShapeDtypeStruct(attn[0].shape, F32)
    ffn_shape = jax.ShapeDtypeStruct(ffn.shape, F32)
    whole = pl.BlockSpec(memory_space=pltpu.VMEM)
    return pl.pallas_call(
        update_kernel,
        in_specs=[pl.BlockSpec(memory_space=pltpu.SMEM)] + [whole] * 11,
        out_specs=[whole] * 8,
        out_shape=[
            attn_shape, attn_shape, attn_shape, ffn_shape, ffn_shape, ffn_shape,
            jax.ShapeDtypeStruct((1, 1), F32), jax.ShapeDtypeStruct((rows, 2), F32),
        ],
        compiler_params=pltpu.CompilerParams(vmem_limit_bytes=VMEM),
        name="update",
    )(rates, squares, gq, go, gk, ffn, *attn, *ffn_state)


ALL = ("dp", "mp")


def shards(
    tokens, cotangent, routes, starts, attn_param, attn_first, attn_second, ffn_param, ffn_first, ffn_second, rates
):
    local_rows, width = tokens.shape
    place = lax.axis_index("mp")
    devices = lax.axis_size("mp")
    groups = lax.axis_size("dp")
    block = local_rows // 2
    manual = groups == 8
    _, depth, cols = ffn_param.shape
    my_x, my_y, my_z = place // 2, lax.axis_index("dp") % 2, lax.axis_index("dp") // 2
    flat = (lax.axis_index("dp") * devices + place).astype(jnp.int32)

    side = jnp.concatenate([routes, starts[:, None] // block], 1).astype(BF16)
    side = jnp.pad(side, ((0, 0), (0, LANES - TOPK - 1)))
    mine = jnp.concatenate([tokens, side], 1)
    sent = halves(mine, place)
    x = deal(mine, sent, place)

    attn_b = attn_param.astype(BF16)
    ffn_b = ffn_param.astype(BF16)
    pad = jnp.zeros((attn_b.shape[0], 2 * LANES - (AC - 2 * SPAN)), BF16)
    wk = jnp.concatenate([attn_b[:, 2 * SPAN :], pad], 1)
    wq = attn_b[:, :SPAN]
    wo = attn_b[:, SPAN : 2 * SPAN]
    if manual:
        wk, wq = after((wk, wq), sent)
        wk = lax.all_to_all(jnp.broadcast_to(wk, (groups * devices, *wk.shape)), ALL, 0, 0, tiled=True)
        wk = wk.reshape(-1, 2 * LANES)
        along = jnp.stack([wq] + [swap_z(wq, turn) for turn in (1, 2, 3)])
        ffn_b, wo = after((ffn_b, wo), along)
        along = jnp.stack([along, swap_y(along)])
        along = after(along, x)
        near = jnp.stack([along, swap_x(along)]).reshape(16, *wq.shape)
        far = swap_core(near)
        chunk = [ffn_b[0].reshape(-1, 16, cols), wo[None, :, :cols], wo[None, :, cols : 2 * cols]]
        chunk += [ffn_b[1].reshape(-1, 16, cols), wo[None, :, 2 * cols :]]
        chunk = gather_z(jnp.concatenate(chunk, 0), my_z)
    else:
        wk = lax.all_gather(wk, ALL, axis=0, tiled=True)
        wq_all = lax.all_gather(wq, ALL, axis=0, tiled=True).reshape(4, 2, 2, 2, 16, -1)
        wq_all = wq_all.transpose(3, 2, 1, 0, 4, 5).reshape(2, 16, 16, -1)
        near, far = wq_all[0], wq_all[1]
        wo_full = lax.all_gather(wo, ALL, axis=0, tiled=True)
        ffn_all = lax.all_gather(ffn_b, ALL, axis=0, tiled=False)
        ffn_all = ffn_all.reshape(groups, devices, 2, depth, cols).transpose(2, 0, 3, 1, 4)
        ffn_all = ffn_all.reshape(2, groups * depth, devices * cols)
        weights = [wo_full, ffn_all[0], ffn_all[1]]

    marks = x[:, width : width + TOPK + 1].astype(jnp.int32)
    x = x[:, :width]
    routes_x = marks[:, :TOPK]
    tile = 128
    tiles = local_rows // tile
    pieces = tiles // 2
    index = jnp.arange(tiles, dtype=jnp.int32)
    low = index < pieces
    here = jnp.where(low, place * block + index * tile, (2 * devices - 1 - place) * block + (index - pieces) * tile)
    lower = jnp.where(low, marks[0, TOPK], marks[block, TOPK]) * block
    where = jnp.stack([here, lower, jnp.full((tiles,), place)]).astype(jnp.int32)

    h, kv, gates = embed_call(x, routes_x, wk)
    kv = kv.reshape(2, block, LANES)
    kv_x = swap_x(kv)
    me = flat.reshape(1) if manual else jnp.zeros((1,), jnp.int32)
    q, wq_full = query_call(me, h, routes_x, near, far)
    if manual:
        a_own = chunk[:, :6]
        b_own = after(chunk[:, 6:], kv_x)
        a_own = jnp.stack([a_own, swap_y(a_own)])
        b_own = jnp.stack([b_own, swap_x(b_own)])
        a_far, b_far = swap_x(a_own), swap_y(b_own)
        weights = [a_own, a_far, b_own, b_far]
        weights += [swap_core(part) for part in weights]
        q = after(q, (a_own, b_own))
    cotangent = after(cotangent, kv_x)
    dy = deal(cotangent, halves(cotangent, place), place)
    o, logs, keys, values = attend_call(where, q, [kv, swap_core(kv), kv_x, swap_core(kv_x)], tile)
    out, dmid, do, deltas, dlogits, gain2, *grads = middle_call(
        groups, flat.reshape(1), x, dy, o, gates, routes_x, wk, weights
    )
    layer_out = gather_back(out, place)

    def back(piece, carried, before):
        return attend_back_call(
            piece, pieces, groups, where, q, do, logs, deltas, routes_x, keys, values, carried, h, before
        )

    all_parts, carried = [], ()
    if manual:
        a_keep, a_send, b_keep, b_send = grads
        moving = (swap_core(a_send), swap_core(b_send))
    for piece in range(pieces - 1):
        all_part, *carried = back(piece, carried, all_parts)
        all_parts.append(all_part)
        if not manual:
            continue
        carried, moving = tied(carried, moving)
        a_in, b_in = moving
        if piece == 0:
            a_now = (a_keep, a_in)
            b_now = (b_keep, b_in)
            turn_a, turn_b, swap_a, swap_b = my_x, my_y, swap_x, swap_y
        elif piece == 1:
            a_now = (a_keep, a_in)
            b_now = (b_keep, b_in)
            turn_a, turn_b, swap_a, swap_b = my_y, my_x, swap_y, swap_x
        if piece < 2:
            a_send = added(at(a_now[0], 1 - turn_a), at(a_now[1], 1 - turn_a))
            b_send = added(at(b_now[0], 1 - turn_b), at(b_now[1], 1 - turn_b))
            a_keep = added(at(a_now[0], turn_a), at(a_now[1], turn_a))
            b_keep = added(at(b_now[0], turn_b), at(b_now[1], turn_b))
            (a_send, b_send, a_keep, b_keep), carried = tied((a_send, b_send, a_keep, b_keep), carried)
            moving = (swap_a(a_send), swap_b(b_send))
        else:
            both = jnp.concatenate([added(a_keep, a_in), added(b_keep, b_in)], 1)
            both, carried = tied(both, carried)
            moving = [swap_z(at(both, my_z ^ turn), turn) for turn in (1, 2, 3)]
            chunk_keep = at(both, my_z)
    all_part, kv_keep, kv_send, gq_keep, gq_send = back(pieces - 1, carried, all_parts)
    all_parts.append(all_part)
    kv_in = swap_core(kv_send)
    kv_out = added(kv_keep[1], kv_in[1])
    kv_keep = added(kv_keep[0], kv_in[0]).reshape(local_rows, LANES)
    kv_recv = swap_x(kv_out).reshape(local_rows, LANES)
    dh = query_back_call(dlogits, wq_full, wk, after(all_parts, (kv_out, kv_keep)))
    if manual:
        gq_in = swap_core(gq_send)
        gq_send = added(at(gq_keep, 1 - my_y), at(gq_in, 1 - my_y))
        gq_keep = added(at(gq_keep, my_y), at(gq_in, my_y))
        gq_y = added(gq_keep, swap_y(gq_send))
        gq = after(gq_y, dh)
        gq_in = [swap_z(at(gq, my_z ^ turn), turn) for turn in (1, 2, 3)]
        gq = sum((part.astype(F32) for part in gq_in), at(gq, my_z).astype(F32)).astype(BF16)
        gq_raw = at(gq, my_x).astype(F32) + swap_x(at(gq, 1 - my_x)).astype(F32)
    grad, gk = post_call(x, h, dmid, dh, kv_keep, kv_recv, dlogits, gain2, wk)
    if manual:
        gk = after(gk, gq_y)
        grad = after(grad, gq)
    input_grad = gather_back(grad, place).astype(F32)

    if manual:
        gk = lax.all_to_all(gk.reshape(groups * devices, -1, 2 * LANES), ALL, 0, 0, tiled=True)
        gk_raw = jnp.sum(gk.astype(F32), 0)
        chunk_raw = sum((part.astype(F32) for part in moving), chunk_keep.astype(F32))
        rows = depth
        ffn_raw = jnp.stack([chunk_raw[:rows], chunk_raw[rows + 32 : 2 * rows + 32]])
        go_raw = jnp.concatenate(
            [chunk_raw[rows : rows + 16], chunk_raw[rows + 16 : rows + 32], chunk_raw[2 * rows + 32 :]], 1
        )
    else:
        g1, g2, go = grads
        ffn_local = jnp.stack([g1, g2]).reshape(2, groups, depth, devices, cols).transpose(1, 3, 0, 2, 4)
        ffn_local = ffn_local.reshape(groups * devices * 2 * depth, cols)
        ffn_raw = lax.psum_scatter(ffn_local, ALL, scatter_dimension=0, tiled=True).astype(F32)
        ffn_raw = ffn_raw.reshape(2, depth, cols)
        go_raw = lax.psum_scatter(go, ALL, scatter_dimension=0, tiled=True).astype(F32)
        gq_raw = lax.psum_scatter(gq_keep, ALL, scatter_dimension=0, tiled=True).astype(F32)
        gk_raw = lax.psum_scatter(gk, ALL, scatter_dimension=0, tiled=True).astype(F32)
    squares = sum(jnp.sum(part * part) for part in (gq_raw, go_raw, gk_raw, ffn_raw))
    if manual:
        squares = jnp.broadcast_to(squares, (groups * devices, 8, LANES))
        squares = lax.all_to_all(squares, ALL, 0, 0, tiled=True)
    else:
        squares = jnp.broadcast_to(lax.psum(squares, ALL), (1, 8, LANES))
    attn_grad, attn_second_new, attn_new, ffn_grad, ffn_second_new, ffn_new, grad_norm, gain_grad = update_call(
        rates, squares, gq_raw, go_raw, gk_raw, ffn_raw,
        (attn_param, attn_first, attn_second), (ffn_param, ffn_first, ffn_second),
    )
    return (
        layer_out,
        input_grad,
        attn_grad,
        attn_second_new,
        attn_new,
        ffn_grad,
        ffn_second_new,
        ffn_new,
        grad_norm.reshape(()),
        gain_grad,
    )


def solution(mesh):
    by_row = P(ALL, None)
    by_ffn = P(None, "dp", "mp")
    return jax.shard_map(
        shards,
        mesh=mesh,
        in_specs=(by_row, by_row, by_row, P(ALL), by_row, by_row, by_row, by_ffn, by_ffn, by_ffn, P()),
        out_specs=(by_row, by_row, by_row, by_row, by_row, by_ffn, by_ffn, by_ffn, P(), by_row),
        check_vma=False,
    )
```

profile of v0, /device:TPU:0, one launch (start us, length us, event | category | flops | bytes accessed | tf_op | source)
XLA Modules:
  0.0 323.2 jit_solution(1055858254448345397)
XLA Ops:
  11.5 3.3 %collective-permute-done.6 = bf16[16,1536]{1,0:T(8,128)(2,1)S(1)} collective-permute-done((bf16[16,1536]{1,0:T(8,128)(2,1)S(1)}, bf16[16,1536]{1,0:T(8,128)(2,1)S(1)}, u32[]{:S(2)}, u32[]{:S(2)}) %collective-permute-start.6) | collective-permute-done | bytes 49184 | tf_op jit(solution)/shard_map/ppermute | solution.py:899
  24.8 3.3 %all-to-all-start = ((bf16[32,16,256]{2,1,0:T(8,128)(2,1)}), bf16[32,16,256]{2,1,0:T(8,128)(2,1)S(1)}, u32[]{:S(2)}, u32[]{:S(2)}) async-start(bf16[32,16,256]{2,1,0:T(8,128)(2,1)} %broadcast_in_dim.25), calls=%async_computation | async-start | bytes 524288 | tf_op jit(solution)/shard_map/all_to_all | solution.py:1022
  30.0 4.3 %collective-permute-done.12 = bf16[11,16,512]{2,1,0:T(8,128)(2,1)S(1)} collective-permute-done((bf16[11,16,512]{2,1,0:T(8,128)(2,1)S(1)}, bf16[11,16,512]{2,1,0:T(8,128)(2,1)S(1)}, u32[]{:S(2)}, u32[]{:S(2)}) %collective-permute-start.12) | collective-permute-done | bytes 180256 | tf_op jit(solution)/shard_map/ppermute | solution.py:899
  45.0 6.4 %embed.1 = (bf16[1024,512]{1,0:T(8,128)(2,1)}, bf16[1024,128]{1,0:T(8,128)(2,1)}, f32[1024,128]{1,0:T(8,128)}) custom-call(bf16[1024,512]{1,0:T(8,128)(2,1)} %fusion.2.x_ref.refs_1_, s32[1024,8]{1,0:T(8,128)} %bitcast.99, bf16[512,256]{1,0:T(8,128)(2,1)} %bitcast.95), custom_call_target="tpu_custom_call" | custom-call | flops 268435456 | bytes 4194304 | tf_op jit(solution)/shard_map/embed/pallas_call | solution.py:135
  55.7 3.8 %collective-permute-done.2.refs_2_ = bf16[2,512,128]{2,1,0:T(8,128)(2,1)} collective-permute-done((bf16[2,512,128]{2,1,0:T(8,128)(2,1)}, bf16[2,512,128]{2,1,0:T(8,128)(2,1)}, u32[]{:S(2)}, u32[]{:S(2)}) %collective-permute-start.2) | collective-permute-done | bytes 262176 | tf_op jit(solution)/shard_map/ppermute | solution.py:891
  66.0 3.8 %collective-permute-done.15 = bf16[4,5,16,512]{3,2,1,0:T(8,128)(2,1)S(1)} collective-permute-done((bf16[4,5,16,512]{3,2,1,0:T(8,128)(2,1)S(1)}, bf16[4,5,16,512]{3,2,1,0:T(8,128)(2,1)S(1)}, u32[]{:S(2)}, u32[]{:S(2)}) %collective-permute-start.15) | collective-permute-done | bytes 327712 | tf_op jit(solution)/shard_map/ppermute | solution.py:891
  75.9 7.6 %query.1 = (bf16[8,1024,128]{2,1,0:T(8,128)(2,1)}, bf16[512,1536]{1,0:T(8,128)(2,1)}) custom-call(s32[1]{0:T(128)} %bitcast.me_ref.refs_0_, bf16[1024,512]{1,0:T(8,128)(2,1)} %get-tuple-element.89.h_ref.refs_9_, s32[1024,8]{1,0:T(8,128)} %bitcast.100, bf16[16,16,1536]{2,1,0:T(8,128)(2,1)} %bitcast.110, bf16[16,16,1536]{2,1,0:T(8,128)(2,1)} %collective-permute-done.10.far_ref), custom_call_target="tpu_custom_call" | custom-call | flops 1610612736 | bytes 5767168 | tf_op jit(solution)/shard_map/query/pallas_call | solution.py:183
  86.8 3.2 collective-permute-start.21
  90.1 17.1 %attend.1 = (f32[8,1024,128]{2,1,0:T(8,128)}, f32[1024,128]{1,0:T(8,128)}, bf16[4096,128]{1,0:T(8,128)(2,1)}, bf16[4096,128]{1,0:T(8,128)(2,1)}) custom-call(s32[3,8]{1,0:T(4,128)} %add_add_fusion.place_ref.refs_0_, bf16[8,1024,128]{2,1,0:T(8,128)(2,1)} %get-tuple-element.96.q_ref.refs_1_, bf16[2,512,128]{2,1,0:T(8,128)(2,1)} %bitcast.2.refs_0_, ...), custom_call_target="tpu_custom_call" | custom-call | flops 34359738368 | bytes 8388608 | tf_op jit(solution)/shard_map/attend/pallas_call | solution.py:319
  109.5 40.4 %middle.1 = (bf16[1024,512]{1,0:T(8,128)(2,1)}, f32[1024,512]{1,0:T(8,128)}, bf16[8,1024,128]{2,1,0:T(8,128)(2,1)}, f32[1024,128]{1,0:T(8,128)}, bf16[1024,128]{...) custom-call(s32[1]{0:T(128)} %bitcast.me_ref.refs_0_, ...), custom_call_target="tpu_custom_call" | custom-call | flops 17716740096 | bytes 8388608 | tf_op jit(solution)/shard_map/middle/pallas_call | solution.py:747
  155.7 10.1 %attend_back.4 = (bf16[256,1536]{1,0:T(8,128)(2,1)}, f32[2,64,4096]{2,1,0:T(8,128)}) custom-call(s32[3,8]{1,0:T(4,128)} %add_add_fusion.place_ref.refs_0_, bf16[8,1024,128]{2,1,0:T(8,128)(2,1)} %get-tuple-element.96.q_ref.refs_1_, bf16[8,1024,128]{2,1,0:T(8,128)(2,1)} %get-tuple-element.103.refs_2_, f32[1024,128]{1,0:T(8,128)} %get-tuple-element.104.refs_3_, ...), custom_call_target="tpu_custom_call" | custom-call | flops 10737418240 | bytes 2097152 | tf_op jit(solution)/shard_map/attend_back/pallas_call | solution.py:507
  170.7 24.6 %collective-permute-start.29 = (bf16[2,4,80,512]{3,2,1,0:T(8,128)(2,1)}, bf16[2,4,80,512]{3,2,1,0:T(8,128)(2,1)S(1)}, u32[]{:S(2)}, u32[]{:S(2)}) collective-permute-start(bf16[2,4,80,512]{3,2,1,0:T(8,128)(2,1)} %get-tuple-element.122), channel_id=1, source_target_pairs={{0,4},{4,0},{8,12},{12,8},{16,20},{20,16},{24,28},{28,24},{1,5},{5... | collective-permute-start | bytes 1966088 | tf_op jit(solution)/shard_map/ppermute | solution.py:895
  195.4 11.5 %attend_back.5 = (bf16[256,1536]{1,0:T(8,128)(2,1)}, f32[2,64,4096]{2,1,0:T(8,128)}) custom-call(s32[3,8]{1,0:T(4,128)} %add_add_fusion.place_ref.refs_0_, bf16[8,1024,128]{2,1,0:T(8,128)(2,1)} %get-tuple-element.96.q_ref.refs_1_, bf16[8,1024,128]{2,1,0:T(8,128)(2,1)} %get-tuple-element.103.refs_2_, f32[1024,128]{1,0:T(8,128)} %get-tuple-element.104.refs_3_, ...), custom_call_target="tpu_custom_call" | custom-call | flops 10737418240 | bytes 2097152 | tf_op jit(solution)/shard_map/attend_back/pallas_call | solution.py:507
  206.9 3.5 %collective-permute-done.29 = bf16[2,4,80,512]{3,2,1,0:T(8,128)(2,1)S(1)} collective-permute-done((bf16[2,4,80,512]{3,2,1,0:T(8,128)(2,1)}, bf16[2,4,80,512]{3,2,1,0:T(8,128)(2,1)S(1)}, u32[]{:S(2)}, u32[]{:S(2)}) %collective-permute-start.29) | collective-permute-done | bytes 655392 | tf_op jit(solution)/shard_map/ppermute | solution.py:895
  210.7 4.4 %collective-permute-start.30 = (bf16[4,96,512]{2,1,0:T(8,128)(2,1)S(1)}, bf16[4,96,512]{2,1,0:T(8,128)(2,1)S(1)}, u32[]{:S(2)}, u32[]{:S(2)}) collective-permute-start(bf16[4,96,512]{2,1,0:T(8,128)(2,1)S(1)} %get-tuple-element.131), channel_id=1, source_target_pairs={{0,4},{4,0},{8,12},{12,8},{16,20},{20,16},{24,28},{28,24},{1,5},{5... | collective-permute-start | bytes 1179656 | tf_op jit(solution)/shard_map/ppermute | solution.py:895
  216.9 11.6 %attend_back.6 = (bf16[256,1536]{1,0:T(8,128)(2,1)}, f32[2,64,4096]{2,1,0:T(8,128)}) custom-call(s32[3,8]{1,0:T(4,128)} %add_add_fusion.place_ref.refs_0_, bf16[8,1024,128]{2,1,0:T(8,128)(2,1)} %get-tuple-element.96.q_ref.refs_1_, bf16[8,1024,128]{2,1,0:T(8,128)(2,1)} %get-tuple-element.103.refs_2_, f32[1024,128]{1,0:T(8,128)} %get-tuple-element.104.refs_3_, ...), custom_call_target="tpu_custom_call" | custom-call | flops 10737418240 | bytes 2097152 | tf_op jit(solution)/shard_map/attend_back/pallas_call | solution.py:507
  228.9 9.5 %collective-permute-start.42 = (bf16[176,512]{1,0:T(8,128)(2,1)S(1)}, bf16[176,512]{1,0:T(8,128)(2,1)S(1)}, u32[]{:S(2)}, u32[]{:S(2)}) collective-permute-start(bf16[176,512]{1,0:T(8,128)(2,1)S(1)} %get-tuple-element.220), channel_id=1, source_target_pairs={{0,8},{4,12},{8,0},{12,4},{16,24},{20,28},{24,16},{28,20},{1,9},{5... | collective-permute-start | bytes 540680 | tf_op jit(solution)/shard_map/ppermute | solution.py:899
  240.8 13.8 %attend_back.7 = (bf16[256,1536]{1,0:T(8,128)(2,1)}, bf16[2,2,512,128]{3,2,1,0:T(8,128)(2,1)}, bf16[2,2,512,128]{3,2,1,0:T(8,128)(2,1)}, bf16[2,4,2,16,1536]{4,3...) custom-call(s32[3,8]{1,0:T(4,128)} %add_add_fusion.place_ref.refs_0_, bf16[8,1024,128]{2,1,0:T(8,128)(2,1)} %get-tuple-element.96.q_ref.refs_1_, ...), custom_call_target="tpu_custom_call" | custom-call | flops 10737418240 | bytes 2097152 | tf_op jit(solution)/shard_map/attend_back/pallas_call | solution.py:507
  257.3 9.8 %collective-permute-start.35 = (bf16[4,2,16,1536]{3,2,1,0:T(8,128)(2,1)S(1)}, bf16[4,2,16,1536]{3,2,1,0:T(8,128)(2,1)S(1)}, u32[]{:S(2)}, u32[]{:S(2)}) collective-permute-start(bf16[4,2,16,1536]{3,2,1,0:T(8,128)(2,1)S(1)} %fusion.11), channel_id=1, source_target_pairs={{0,4},{4,0},{8,12},{12,8},{16,20},{20,16},{24,28},{28,24},{1,5},{5... | collective-permute-start | bytes 1179656 | tf_op jit(solution)/shard_map/ppermute | solution.py:895
  268.4 5.8 %query_back.1.dh_ref = f32[1024,512]{1,0:T(8,128)} custom-call(bf16[1024,128]{1,0:T(8,128)(2,1)} %get-tuple-element.101.dlog_ref, bf16[512,1536]{1,0:T(8,128)(2,1)} %get-tuple-element.102.wq_ref, bf16[512,256]{1,0:T(8,128)(2,1)} %bitcast.97, bf16[256,1536]{1,0:T(8,128)(2,1)} %get-tuple-element.141.refs_10_.refs_0_, ...), custom_call_target="tpu_custom_call" | custom-call | flops 1744830464 | bytes 8388608 | tf_op jit(solution)/shard_map/query_back/pallas_call | solution.py:541
  277.9 3.3 %collective-permute-start.38 = (bf16[2,16,1536]{2,1,0:T(8,128)(2,1)S(1)}, bf16[2,16,1536]{2,1,0:T(8,128)(2,1)S(1)}, u32[]{:S(2)}, u32[]{:S(2)}) collective-permute-start(bf16[2,16,1536]{2,1,0:T(8,128)(2,1)S(1)} %get-tuple-element.232), channel_id=1, source_target_pairs={{0,24},{4,28},{8,16},{12,20},{16,8},{20,12},{24,0},{28,4},{1,25},{... | collective-permute-start | bytes 294920 | tf_op jit(solution)/shard_map/ppermute | solution.py:899
  283.2 6.7 %finish.1 = (bf16[1024,512]{1,0:T(8,128)(2,1)}, bf16[512,256]{1,0:T(8,128)(2,1)}) custom-call(bf16[1024,512]{1,0:T(8,128)(2,1)} %fusion.2.x_ref.refs_1_, bf16[1024,512]{1,0:T(8,128)(2,1)} %get-tuple-element.89.h_ref.refs_9_, f32[1024,512]{1,0:T(8,128)} %get-tuple-element.100.dmid_ref, f32[1024,512]{1,0:T(8,128)} %query_back.1.dh_ref, ...), custom_call_target="tpu_custom_call" | custom-call | flops 402653184 | bytes 8388608 | tf_op jit(solution)/shard_map/finish/pallas_call | solution.py:829
  305.9 3.8 %all-to-all-start.2 = ((f32[32,8,128]{2,1,0:T(8,128)}), f32[32,8,128]{2,1,0:T(8,128)S(1)}, u32[]{:S(2)}, u32[]{:S(2)}) async-start(f32[32,8,128]{2,1,0:T(8,128)} %broadcast_in_dim.31), calls=%async_computation.2 | async-start | bytes 262144 | tf_op jit(solution)/shard_map/all_to_all | solution.py:1157
  311.5 6.5 %all-to-all-done.2.squares_ref = f32[32,8,128]{2,1,0:T(8,128)S(1)} async-done(((f32[32,8,128]{2,1,0:T(8,128)}), f32[32,8,128]{2,1,0:T(8,128)S(1)}, u32[]{:S(2)}, u32[]{:S(2)}) %all-to-all-start.2) | async-done | bytes 131104 | tf_op jit(solution)/shard_map/all_to_all | solution.py:1157
  (192 shorter events, 100.6 us)
Async XLA Ops:
  18.2 16.1 %collective-permute-start.12 = (bf16[11,16,512]{2,1,0:T(8,128)(2,1)S(1)}, bf16[11,16,512]{2,1,0:T(8,128)(2,1)S(1)}, u32[]{:S(2)}, u32[]{:S(2)}) collective-permute-start(bf16[11,16,512]{2,1,0:T(8,128)(2,1)S(1)} %bitcast_dynamic-update-slice_fusion), channel_id=1, source_target_pairs={{0,16},{4,20},{8,24},{12,28},{16,0},{20,4},{24,8},{28,12},{1,17},{... | collective-permute-start | bytes 540680 | tf_op jit(solution)/shard_map/ppermute | solution.py:899
  22.6 17.0 %collective-permute-start = (bf16[512,640]{1,0:T(8,128)(2,1)}, bf16[512,640]{1,0:T(8,128)(2,1)}, u32[]{:S(2)}, u32[]{:S(2)}) collective-permute-start(bf16[512,640]{1,0:T(8,128)(2,1)} %get-tuple-element.211), channel_id=1, source_target_pairs={{1,3},{3,1},{5,7},{7,5},{9,11},{11,9},{13,15},{15,13},{17,19},{19,... | collective-permute-start | bytes 1966088 | tf_op jit(solution)/shard_map/ppermute | solution.py:866
  24.1 16.9 %collective-permute-start.1 = (bf16[512,640]{1,0:T(8,128)(2,1)}, bf16[512,640]{1,0:T(8,128)(2,1)}, u32[]{:S(2)}, u32[]{:S(2)}) collective-permute-start(bf16[512,640]{1,0:T(8,128)(2,1)} %get-tuple-element.210), channel_id=1, source_target_pairs={{0,1},{1,2},{2,3},{3,0},{4,5},{5,6},{6,7},{7,4},{8,9},{9,10},{10,1... | collective-permute-start | bytes 1966088 | tf_op jit(solution)/shard_map/ppermute | solution.py:865
  24.8 19.5 %all-to-all-start = ((bf16[32,16,256]{2,1,0:T(8,128)(2,1)}), bf16[32,16,256]{2,1,0:T(8,128)(2,1)S(1)}, u32[]{:S(2)}, u32[]{:S(2)}) async-start(bf16[32,16,256]{2,1,0:T(8,128)(2,1)} %broadcast_in_dim.25), calls=%async_computation | async-start | bytes 524288 | tf_op jit(solution)/shard_map/all_to_all | solution.py:1022
  38.1 21.8 %collective-permute-start.9 = (bf16[2,4,16,1536]{3,2,1,0:T(8,128)(2,1)S(1)}, bf16[2,4,16,1536]{3,2,1,0:T(8,128)(2,1)}, u32[]{:S(2)}, u32[]{:S(2)}) collective-permute-start(bf16[2,4,16,1536]{3,2,1,0:T(8,128)(2,1)S(1)} %pad_maximum_fusion.8), channel_id=1, source_target_pairs={{0,2},{2,0},{1,3},{3,1},{4,6},{6,4},{5,7},{7,5},{8,10},{10,8},{9,1... | collective-permute-start | bytes 1179656 | tf_op jit(solution)/shard_map/ppermute | solution.py:891
  64.2 22.6 %collective-permute-start.18 = (bf16[2,4,6,16,512]{4,3,2,1,0:T(8,128)(2,1)S(1)}, bf16[2,4,6,16,512]{4,3,2,1,0:T(8,128)(2,1)}, u32[]{:S(2)}, u32[]{:S(2)}) collective-permute-start(bf16[2,4,6,16,512]{4,3,2,1,0:T(8,128)(2,1)S(1)} %pad_maximum_fusion.4.refs_7_), channel_id=1, source_target_pairs={{0,2},{2,0},{1,3},{3,1},{4,6},{6,4},{5,7},{7,5},{8,10},{10,8},{9,1... | collective-permute-start | bytes 2359304 | tf_op jit(solution)/shard_map/ppermute | solution.py:891
  69.9 20.1 %collective-permute-start.19 = (bf16[2,4,5,16,512]{4,3,2,1,0:T(8,128)(2,1)S(1)}, bf16[2,4,5,16,512]{4,3,2,1,0:T(8,128)(2,1)S(1)}, u32[]{:S(2)}, u32[]{:S(2)}) collective-permute-start(bf16[2,4,5,16,512]{4,3,2,1,0:T(8,128)(2,1)S(1)} %pad_maximum_fusion.7.refs_9_), channel_id=1, source_target_pairs={{0,4},{4,0},{8,12},{12,8},{16,20},{20,16},{24,28},{28,24},{1,5},{5... | collective-permute-start | bytes 1966088 | tf_op jit(solution)/shard_map/ppermute | solution.py:895
  71.4 15.4 %collective-permute-start.3 = (bf16[512,512]{1,0:T(8,128)(2,1)S(1)}, bf16[512,512]{1,0:T(8,128)(2,1)S(1)}, u32[]{:S(2)}, u32[]{:S(2)}) collective-permute-start(bf16[512,512]{1,0:T(8,128)(2,1)S(1)} %get-tuple-element.219), channel_id=1, source_target_pairs={{1,3},{3,1},{5,7},{7,5},{9,11},{11,9},{13,15},{15,13},{17,19},{19,... | collective-permute-start | bytes 1572872 | tf_op jit(solution)/shard_map/ppermute | solution.py:866
  83.5 24.9 %collective-permute-start.20 = (bf16[2,4,6,16,512]{4,3,2,1,0:T(8,128)(2,1)S(1)}, bf16[2,4,6,16,512]{4,3,2,1,0:T(8,128)(2,1)S(1)}, u32[]{:S(2)}, u32[]{:S(2)}) collective-permute-start(bf16[2,4,6,16,512]{4,3,2,1,0:T(8,128)(2,1)S(1)} %pad_maximum_fusion.4.refs_7_), channel_id=1, source_target_pairs={{0,1},{1,0},{2,3},{3,2},{4,5},{5,4},{6,7},{7,6},{8,9},{9,8},{10,11... | collective-permute-start | bytes 2359304 | tf_op jit(solution)/shard_map/ppermute | solution.py:887
  84.3 22.9 %collective-permute-start.4 = (bf16[512,512]{1,0:T(8,128)(2,1)S(1)}, bf16[512,512]{1,0:T(8,128)(2,1)S(1)}, u32[]{:S(2)}, u32[]{:S(2)}) collective-permute-start(bf16[512,512]{1,0:T(8,128)(2,1)S(1)} %get-tuple-element.218), channel_id=1, source_target_pairs={{0,1},{1,2},{2,3},{3,0},{4,5},{5,6},{6,7},{7,4},{8,9},{9,10},{10,1... | collective-permute-start | bytes 1572872 | tf_op jit(solution)/shard_map/ppermute | solution.py:865
  86.8 21.6 %collective-permute-start.22 = (bf16[2,4,5,16,512]{4,3,2,1,0:T(8,128)(2,1)S(1)}, bf16[2,4,5,16,512]{4,3,2,1,0:T(8,128)(2,1)}, u32[]{:S(2)}, u32[]{:S(2)}) collective-permute-start(bf16[2,4,5,16,512]{4,3,2,1,0:T(8,128)(2,1)S(1)} %pad_maximum_fusion.7.refs_9_), channel_id=1, source_target_pairs={{0,1},{1,0},{2,3},{3,2},{4,5},{5,4},{6,7},{7,6},{8,9},{9,8},{10,11... | collective-permute-start | bytes 1966088 | tf_op jit(solution)/shard_map/ppermute | solution.py:887
  86.8 21.6 %collective-permute-start.21 = (bf16[2,4,6,16,512]{4,3,2,1,0:T(8,128)(2,1)}, bf16[2,4,6,16,512]{4,3,2,1,0:T(8,128)(2,1)}, u32[]{:S(2)}, u32[]{:S(2)}) collective-permute-start(bf16[2,4,6,16,512]{4,3,2,1,0:T(8,128)(2,1)} %collective-permute-done.18.refs_8_), channel_id=1, source_target_pairs={{0,1},{1,0},{2,3},{3,2},{4,5},{5,4},{6,7},{7,6},{8,9},{9,8},{10,11... | collective-permute-start | bytes 2359304 | tf_op jit(solution)/shard_map/ppermute | solution.py:887
  90.0 18.4 %collective-permute-start.23 = (bf16[2,4,5,16,512]{4,3,2,1,0:T(8,128)(2,1)S(1)}, bf16[2,4,5,16,512]{4,3,2,1,0:T(8,128)(2,1)S(1)}, u32[]{:S(2)}, u32[]{:S(2)}) collective-permute-start(bf16[2,4,5,16,512]{4,3,2,1,0:T(8,128)(2,1)S(1)} %collective-permute-done.19.refs_10_), channel_id=1, source_target_pairs={{0,1},{1,0},{2,3},{3,2},{4,5},{5,4},{6,7},{7,6},{8,9},{9,8},{10,11... | collective-permute-start | bytes 1966088 | tf_op jit(solution)/shard_map/ppermute | solution.py:887
  150.0 17.2 %collective-permute-start.26 = (bf16[2,2,4,96,512]{4,3,2,1,0:T(8,128)(2,1)}, bf16[2,2,4,96,512]{4,3,2,1,0:T(8,128)(2,1)S(1)}, u32[]{:S(2)}, u32[]{:S(2)}) collective-permute-start(bf16[2,2,4,96,512]{4,3,2,1,0:T(8,128)(2,1)} %get-tuple-element.111), channel_id=1, source_target_pairs={{0,1},{1,0},{2,3},{3,2},{4,5},{5,4},{6,7},{7,6},{8,9},{9,8},{10,11... | collective-permute-start | bytes 4718600 | tf_op jit(solution)/shard_map/ppermute | solution.py:887
  150.5 16.7 %collective-permute-start.27 = (bf16[2,2,4,80,512]{4,3,2,1,0:T(8,128)(2,1)}, bf16[2,2,4,80,512]{4,3,2,1,0:T(8,128)(2,1)S(1)}, u32[]{:S(2)}, u32[]{:S(2)}) collective-permute-start(bf16[2,2,4,80,512]{4,3,2,1,0:T(8,128)(2,1)} %get-tuple-element.112), channel_id=1, source_target_pairs={{0,1},{1,0},{2,3},{3,2},{4,5},{5,4},{6,7},{7,6},{8,9},{9,8},{10,11... | collective-permute-start | bytes 3932168 | tf_op jit(solution)/shard_map/ppermute | solution.py:887
  169.4 40.9 %collective-permute-start.28 = (bf16[2,4,96,512]{3,2,1,0:T(8,128)(2,1)S(1)}, bf16[2,4,96,512]{3,2,1,0:T(8,128)(2,1)S(1)}, u32[]{:S(2)}, u32[]{:S(2)}) collective-permute-start(bf16[2,4,96,512]{3,2,1,0:T(8,128)(2,1)S(1)} %get-tuple-element.121), channel_id=1, source_target_pairs={{0,2},{2,0},{1,3},{3,1},{4,6},{6,4},{5,7},{7,5},{8,10},{10,8},{9,1... | collective-permute-start | bytes 2359304 | tf_op jit(solution)/shard_map/ppermute | solution.py:891
  170.7 39.6 %collective-permute-start.29 = (bf16[2,4,80,512]{3,2,1,0:T(8,128)(2,1)}, bf16[2,4,80,512]{3,2,1,0:T(8,128)(2,1)S(1)}, u32[]{:S(2)}, u32[]{:S(2)}) collective-permute-start(bf16[2,4,80,512]{3,2,1,0:T(8,128)(2,1)} %get-tuple-element.122), channel_id=1, source_target_pairs={{0,4},{4,0},{8,12},{12,8},{16,20},{20,16},{24,28},{28,24},{1,5},{5... | collective-permute-start | bytes 1966088 | tf_op jit(solution)/shard_map/ppermute | solution.py:895
  210.7 17.8 %collective-permute-start.30 = (bf16[4,96,512]{2,1,0:T(8,128)(2,1)S(1)}, bf16[4,96,512]{2,1,0:T(8,128)(2,1)S(1)}, u32[]{:S(2)}, u32[]{:S(2)}) collective-permute-start(bf16[4,96,512]{2,1,0:T(8,128)(2,1)S(1)} %get-tuple-element.131), channel_id=1, source_target_pairs={{0,4},{4,0},{8,12},{12,8},{16,20},{20,16},{24,28},{28,24},{1,5},{5... | collective-permute-start | bytes 1179656 | tf_op jit(solution)/shard_map/ppermute | solution.py:895
  228.9 27.4 %collective-permute-start.42 = (bf16[176,512]{1,0:T(8,128)(2,1)S(1)}, bf16[176,512]{1,0:T(8,128)(2,1)S(1)}, u32[]{:S(2)}, u32[]{:S(2)}) collective-permute-start(bf16[176,512]{1,0:T(8,128)(2,1)S(1)} %get-tuple-element.220), channel_id=1, source_target_pairs={{0,8},{4,12},{8,0},{12,4},{16,24},{20,28},{24,16},{28,20},{1,9},{5... | collective-permute-start | bytes 540680 | tf_op jit(solution)/shard_map/ppermute | solution.py:899
  238.4 17.9 %collective-permute-start.43 = (bf16[176,512]{1,0:T(8,128)(2,1)S(1)}, bf16[176,512]{1,0:T(8,128)(2,1)S(1)}, u32[]{:S(2)}, u32[]{:S(2)}) collective-permute-start(bf16[176,512]{1,0:T(8,128)(2,1)S(1)} %get-tuple-element.222), channel_id=1, source_target_pairs={{0,16},{4,20},{8,24},{12,28},{16,0},{20,4},{24,8},{28,12},{1,17},{... | collective-permute-start | bytes 540680 | tf_op jit(solution)/shard_map/ppermute | solution.py:899
  238.4 17.9 %collective-permute-start.44 = (bf16[176,512]{1,0:T(8,128)(2,1)S(1)}, bf16[176,512]{1,0:T(8,128)(2,1)S(1)}, u32[]{:S(2)}, u32[]{:S(2)}) collective-permute-start(bf16[176,512]{1,0:T(8,128)(2,1)S(1)} %get-tuple-element.221), channel_id=1, source_target_pairs={{0,24},{4,28},{8,16},{12,20},{16,8},{20,12},{24,0},{28,4},{1,25},{... | collective-permute-start | bytes 540680 | tf_op jit(solution)/shard_map/ppermute | solution.py:899
  257.3 19.2 %collective-permute-start.35 = (bf16[4,2,16,1536]{3,2,1,0:T(8,128)(2,1)S(1)}, bf16[4,2,16,1536]{3,2,1,0:T(8,128)(2,1)S(1)}, u32[]{:S(2)}, u32[]{:S(2)}) collective-permute-start(bf16[4,2,16,1536]{3,2,1,0:T(8,128)(2,1)S(1)} %fusion.11), channel_id=1, source_target_pairs={{0,4},{4,0},{8,12},{12,8},{16,20},{20,16},{24,28},{28,24},{1,5},{5... | collective-permute-start | bytes 1179656 | tf_op jit(solution)/shard_map/ppermute | solution.py:895
  276.7 16.0 %collective-permute-start.36 = (bf16[2,16,1536]{2,1,0:T(8,128)(2,1)S(1)}, bf16[2,16,1536]{2,1,0:T(8,128)(2,1)S(1)}, u32[]{:S(2)}, u32[]{:S(2)}) collective-permute-start(bf16[2,16,1536]{2,1,0:T(8,128)(2,1)S(1)} %get-tuple-element.231), channel_id=1, source_target_pairs={{0,8},{4,12},{8,0},{12,4},{16,24},{20,28},{24,16},{28,20},{1,9},{5... | collective-permute-start | bytes 294920 | tf_op jit(solution)/shard_map/ppermute | solution.py:899
  277.9 14.9 %collective-permute-start.38 = (bf16[2,16,1536]{2,1,0:T(8,128)(2,1)S(1)}, bf16[2,16,1536]{2,1,0:T(8,128)(2,1)S(1)}, u32[]{:S(2)}, u32[]{:S(2)}) collective-permute-start(bf16[2,16,1536]{2,1,0:T(8,128)(2,1)S(1)} %get-tuple-element.232), channel_id=1, source_target_pairs={{0,24},{4,28},{8,16},{12,20},{16,8},{20,12},{24,0},{28,4},{1,25},{... | collective-permute-start | bytes 294920 | tf_op jit(solution)/shard_map/ppermute | solution.py:899
  (44 other events, 380.9 us)
where the time goes:
time: 330 us; the launch traced here: 323 us
  Pallas kernels  134 us (41%)
  starting transfers between devices  106 us (32%)
  waiting for transfers between devices  39.6 us (12%)
  other arithmetic  26.5 us (8%)
  local copies, waits for them, and re-layouts  13 us (4%)
  between operations  4.3 us (1%)
    pallas_call x4, Pallas kernels, attend_back_call(): pl.pallas_call(functools.partial(attend_back_kernel, piece, pieces, group...  47.1 us
    ppermute x6, starting transfers between devices, swap_y(): return lax.ppermute(values, 'dp', tuple(((i, i ^ 1) for i in range(8))))  43.6 us
    pallas_call x1, Pallas kernels, middle_call(): pl.pallas_call(functools.partial(middle_kernel, groups), grid_spec=pltpu....  40.4 us
    ppermute x12, starting transfers between devices, swap_z(): lax.ppermute(values, 'dp', tuple(((i, i ^ 2 * turn) for i in range(8))))  26.4 us
    pallas_call x1, Pallas kernels, attend_call(): pl.pallas_call(attend_kernel, grid_spec=pltpu.PrefetchScalarGridSpec(num_...  17.1 us
    ppermute x8, starting transfers between devices, swap_x(): return lax.ppermute(values, 'mp', OTHER_X)  10.8 us
    ppermute x6, waiting for transfers between devices, swap_y(): return lax.ppermute(values, 'dp', tuple(((i, i ^ 1) for i in range(8))))  10.4 us
    ppermute x12, waiting for transfers between devices, swap_z(): lax.ppermute(values, 'dp', tuple(((i, i ^ 2 * turn) for i in range(8))))  10.2 us
  transfers between devices with their start and end apart: 48, of which 14 were waited for; matrix products, arithmetic and copies ran while one was open for 8% of the time, Pallas kernels for 28%

commit v1 on v0

--- a/solution.py
+++ b/solution.py
@@ -142,7 +142,7 @@
             jax.ShapeDtypeStruct((rows, LANES), BF16),
             jax.ShapeDtypeStruct((rows, LANES), F32),
         ],
-        compiler_params=pltpu.CompilerParams(vmem_limit_bytes=VMEM),
+        compiler_params=pltpu.CompilerParams(vmem_limit_bytes=12 << 20),
         cost_estimate=pl.CostEstimate(
             flops=4 * rows * width * LANES, bytes_accessed=8 * rows * width, transcendentals=0
         ),
@@ -201,7 +201,7 @@
             jax.ShapeDtypeStruct((TOPK, rows, LANES), BF16),
             jax.ShapeDtypeStruct((width, cols), BF16),
         ],
-        compiler_params=pltpu.CompilerParams(vmem_limit_bytes=VMEM),
+        compiler_params=pltpu.CompilerParams(vmem_limit_bytes=16 << 20),
         cost_estimate=pl.CostEstimate(
             flops=2 * rows * width * cols, bytes_accessed=8 * rows * width + 2 * width * cols, transcendentals=0
         ),
@@ -344,7 +344,7 @@
             jax.ShapeDtypeStruct((count, LANES), BF16),
             jax.ShapeDtypeStruct((count, LANES), BF16),
         ],
-        compiler_params=pltpu.CompilerParams(vmem_limit_bytes=VMEM),
+        compiler_params=pltpu.CompilerParams(vmem_limit_bytes=24 << 20),
         cost_estimate=pl.CostEstimate(
             flops=8 * slots * rows * count * LANES, bytes_accessed=8 * slots * rows * LANES, transcendentals=0
         ),
@@ -371,26 +371,27 @@
     rows = slots * tile
     width = 512
 
+    def carry_copies():
+        return [
+            pltpu.make_async_copy(sums_in.at[0], dkey_ref.at[pl.ds(0, HD), :], sems.at[0]),
+            pltpu.make_async_copy(sums_in.at[1], dvalue_ref.at[pl.ds(0, HD), :], sems.at[1]),
+        ]
+
     @pl.when(step == 0)
     def _():
-        dkey_ref[...] = jnp.zeros_like(dkey_ref)
-        dvalue_ref[...] = jnp.zeros_like(dvalue_ref)
-        if not first:
-            copies = [
-                pltpu.make_async_copy(sums_in.at[0], dkey_ref.at[pl.ds(0, HD), :], sems.at[0]),
-                pltpu.make_async_copy(sums_in.at[1], dvalue_ref.at[pl.ds(0, HD), :], sems.at[1]),
-            ]
-            for copy in copies:
+        if first:
+            dkey_ref[:HD] = jnp.zeros_like(dkey_ref[:HD])
+            dvalue_ref[:HD] = jnp.zeros_like(dvalue_ref[:HD])
+        else:
+            for copy in carry_copies():
                 copy.start()
-            for copy in copies:
-                copy.wait()
+        dkey_ref[HD:] = jnp.zeros_like(dkey_ref[HD:])
+        dvalue_ref[HD:] = jnp.zeros_like(dvalue_ref[HD:])
 
     here = place_ref[0, piece + pieces * step]
     lower = place_ref[1, piece + pieces * step]
     q = q_ref[...].reshape(rows, LANES)
     do = do_ref[...].reshape(rows, LANES)
-    q_turned = turned(q)
-    do_turned = turned(do)
     logs = log_ref[...]
     deltas = delta_ref[...]
     logs = jnp.concatenate([column(logs, slot, tile) for slot in range(slots)], 0)
@@ -404,6 +405,13 @@
     def wide(values):
         return jnp.concatenate([values] * (width // LANES), 1)
 
+    if not first:
+
+        @pl.when(step == 0)
+        def _():
+            for copy in carry_copies():
+                copy.wait()
+
     def one(start, masked):
         span = pl.ds(start, width)
         keys = key_ref[span, :]
@@ -413,8 +421,8 @@
             probs = jnp.where(allowed, probs, 0.0)
         dprobs = dot_last(do, value_ref[span, :])
         dscores = (probs * (dprobs - wide(deltas))).astype(BF16)
-        dvalue_ref[:, span] += dot(do_turned, probs.astype(BF16))
-        dkey_ref[:, span] += dot(q_turned, dscores)
+        dvalue_ref[:, span] += dot_first(do, probs.astype(BF16))
+        dkey_ref[:, span] += dot_first(q, dscores)
         return dot(dscores, keys)
 
     dq_ref[...] = one(last, True)
@@ -425,6 +433,21 @@
 
     lax.fori_loop(0, full, body, 0)
 
+    def sum_copies():
+        return [
+            pltpu.make_async_copy(dkey_ref.at[pl.ds(0, HD), :], outs[0].at[0], sems.at[0]),
+            pltpu.make_async_copy(dvalue_ref.at[pl.ds(0, HD), :], outs[0].at[1], sems.at[1]),
+        ]
+
+    if not final:
+
+        @pl.when(step == steps - 1)
+        def _():
+            dkey_ref[:HD] += dkey_ref[HD:]
+            dvalue_ref[:HD] += dvalue_ref[HD:]
+            for copy in sum_copies():
+                copy.start()
+
     dq = (dq_ref[...] * SCALE).astype(BF16).reshape(slots, tile, LANES)
     mine = pl.ds(pl.multiple_of(step * tile, tile), tile)
     all_ref[mine, :] = place_pairs([dq[slot] for slot in range(slots)], choices(routes_ref[...], tile, BF16))
@@ -432,15 +455,7 @@
     @pl.when(step == steps - 1)
     def _():
         if not final:
-            dkey_ref[:HD] += dkey_ref[HD:]
-            dvalue_ref[:HD] += dvalue_ref[HD:]
-            copies = [
-                pltpu.make_async_copy(dkey_ref.at[pl.ds(0, HD), :], outs[0].at[0], sems.at[0]),
-                pltpu.make_async_copy(dvalue_ref.at[pl.ds(0, HD), :], outs[0].at[1], sems.at[1]),
-            ]
-            for copy in copies:
-                copy.start()
-            for copy in copies:
+            for copy in sum_copies():
                 copy.wait()
             return
         kv_keep, kv_send, gq_keep, gq_send = outs
@@ -519,7 +534,7 @@
             ],
         ),
         out_shape=out_shape,
-        compiler_params=pltpu.CompilerParams(vmem_limit_bytes=VMEM),
+        compiler_params=pltpu.CompilerParams(vmem_limit_bytes=20 << 20),
         cost_estimate=pl.CostEstimate(
             flops=10 * slots * 2 * tile * count * LANES, bytes_accessed=16 * slots * tile * LANES, transcendentals=0
         ),
@@ -546,7 +561,7 @@
         ],
         out_specs=whole((rows, width)),
         out_shape=jax.ShapeDtypeStruct((rows, width), F32),
-        compiler_params=pltpu.CompilerParams(vmem_limit_bytes=VMEM),
+        compiler_params=pltpu.CompilerParams(vmem_limit_bytes=24 << 20),
         cost_estimate=pl.CostEstimate(
             flops=2 * rows * width * (SPAN + LANES), bytes_accessed=4 * rows * (SPAN + width), transcendentals=0
         ),
@@ -784,7 +799,7 @@
             jax.ShapeDtypeStruct((1, width), F32),
             *[jax.ShapeDtypeStruct(shape, BF16) for shape in grads],
         ],
-        compiler_params=pltpu.CompilerParams(vmem_limit_bytes=VMEM),
+        compiler_params=pltpu.CompilerParams(vmem_limit_bytes=48 << 20),
         cost_estimate=pl.CostEstimate(
             flops=2 * rows * width * (6 * hidden + 3 * SPAN), bytes_accessed=16 * rows * width, transcendentals=0
         ),
@@ -840,7 +855,7 @@
             jax.ShapeDtypeStruct((width, 2 * LANES), BF16),
         ],
         scratch_shapes=[pltpu.VMEM((width, 2 * LANES), F32)],
-        compiler_params=pltpu.CompilerParams(vmem_limit_bytes=VMEM),
+        compiler_params=pltpu.CompilerParams(vmem_limit_bytes=16 << 20),
         cost_estimate=pl.CostEstimate(
             flops=6 * rows * width * LANES, bytes_accessed=16 * rows * width, transcendentals=0
         ),
@@ -860,10 +875,12 @@
     return first, second
 
 
-def deal(rows, sent, place):
+def deal(rows, sent, place, ready=None):
     half = rows.shape[0] // 2
     ring = lax.ppermute(sent[0], "mp", RING)
     swap = lax.ppermute(sent[1], "mp", SWAP)
+    if ready is not None:
+        ring, swap = after((ring, swap), ready)
     low = jnp.where(place == 0, rows[:half], jnp.where(place == 3, swap, ring))
     high = jnp.where(place == 2, rows[half:], jnp.where(place == 1, swap, ring))
     return jnp.concatenate([low, high], 0)
@@ -984,7 +1001,7 @@
             attn_shape, attn_shape, attn_shape, ffn_shape, ffn_shape, ffn_shape,
             jax.ShapeDtypeStruct((1, 1), F32), jax.ShapeDtypeStruct((rows, 2), F32),
         ],
-        compiler_params=pltpu.CompilerParams(vmem_limit_bytes=VMEM),
+        compiler_params=pltpu.CompilerParams(vmem_limit_bytes=24 << 20),
         name="update",
     )(rates, squares, gq, go, gk, ffn, *attn, *ffn_state)
 
@@ -1023,8 +1040,8 @@
         wk = wk.reshape(-1, 2 * LANES)
         along = jnp.stack([wq] + [swap_z(wq, turn) for turn in (1, 2, 3)])
         ffn_b, wo = after((ffn_b, wo), along)
+        along = after(along, x)
         along = jnp.stack([along, swap_y(along)])
-        along = after(along, x)
         near = jnp.stack([along, swap_x(along)]).reshape(16, *wq.shape)
         far = swap_core(near)
         chunk = [ffn_b[0].reshape(-1, 16, cols), wo[None, :, :cols], wo[None, :, cols : 2 * cols]]
@@ -1057,19 +1074,25 @@
     kv = kv.reshape(2, block, LANES)
     kv_x = swap_x(kv)
     me = flat.reshape(1) if manual else jnp.zeros((1,), jnp.int32)
-    q, wq_full = query_call(me, h, routes_x, near, far)
     if manual:
+        chunk = after(chunk, kv)
         a_own = chunk[:, :6]
-        b_own = after(chunk[:, 6:], kv_x)
+        b_own = chunk[:, 6:]
         a_own = jnp.stack([a_own, swap_y(a_own)])
         b_own = jnp.stack([b_own, swap_x(b_own)])
         a_far, b_far = swap_x(a_own), swap_y(b_own)
         weights = [a_own, a_far, b_own, b_far]
-        weights += [swap_core(part) for part in weights]
-        q = after(q, (a_own, b_own))
-    cotangent = after(cotangent, kv_x)
-    dy = deal(cotangent, halves(cotangent, place), place)
+        near, far = after((near, far), (a_own, b_own))
+    q, wq_full = query_call(me, h, routes_x, near, far)
     o, logs, keys, values = attend_call(where, q, [kv, swap_core(kv), kv_x, swap_core(kv_x)], tile)
+    if manual:
+        own = [swap_core(a_own), swap_core(b_own)]
+        a_far, b_far = after((a_far, b_far), logs)
+        weights += [own[0], swap_core(a_far), own[1], swap_core(b_far)]
+        cotangent = after(cotangent, (q, own))
+    else:
+        cotangent = after(cotangent, q)
+    dy = deal(cotangent, halves(cotangent, place), place, logs)
     out, dmid, do, deltas, dlogits, gain2, *grads = middle_call(
         groups, flat.reshape(1), x, dy, o, gates, routes_x, wk, weights
     )
@@ -1129,7 +1152,7 @@
         gq_raw = at(gq, my_x).astype(F32) + swap_x(at(gq, 1 - my_x)).astype(F32)
     grad, gk = post_call(x, h, dmid, dh, kv_keep, kv_recv, dlogits, gain2, wk)
     if manual:
-        gk = after(gk, gq_y)
+        gk = after(gk, gq)
         grad = after(grad, gq)
     input_grad = gather_back(grad, place).astype(F32)
 

time: 330 us -> 306 us (0.927)
  the two profiles are of different devices: /device:TPU:0 before, /device:TPU:1 now
where the time goes in v1:
time: 306 us; the launch traced here: 300 us
  Pallas kernels  99.4 us (32%)
  starting transfers between devices  98.5 us (32%)
  waiting for transfers between devices  56.4 us (18%)
  local copies, waits for them, and re-layouts  21.4 us (7%)
  other arithmetic  20.1 us (7%)
  between operations  4.51 us (1%)
    pallas_call x1, Pallas kernels, middle_call(): pl.pallas_call(functools.partial(middle_kernel, groups), grid_spec=pltpu....  38.2 us
    ppermute x6, starting transfers between devices, swap_y(): return lax.ppermute(values, 'dp', tuple(((i, i ^ 1) for i in range(8))))  35.2 us
    pallas_call x4, Pallas kernels, attend_back_call(): pl.pallas_call(functools.partial(attend_back_kernel, piece, pieces, group...  28 us
    ppermute x6, waiting for transfers between devices, swap_y(): return lax.ppermute(values, 'dp', tuple(((i, i ^ 1) for i in range(8))))  24.6 us
    ppermute x12, starting transfers between devices, swap_z(): lax.ppermute(values, 'dp', tuple(((i, i ^ 2 * turn) for i in range(8))))  19.1 us
    unnamed x97, local copies, waits for them, and re-layouts  14.7 us
    pallas_call x1, Pallas kernels, attend_call(): pl.pallas_call(attend_kernel, grid_spec=pltpu.PrefetchScalarGridSpec(num_...  14.4 us
    ppermute x11, starting transfers between devices, swap_core(): return lax.ppermute(values, 'mp', OTHER_CORE)  10.4 us
  transfers between devices with their start and end apart: 48, of which 18 were waited for; matrix products, arithmetic and copies ran while one was open for 6% of the time, Pallas kernels for 20%

profile of v1, /device:TPU:1, one launch (start us, length us, event | category | flops | bytes accessed | tf_op | source)
XLA Modules:
  0.0 300.3 jit_solution(10284964302070997484)
XLA Ops:
  15.8 3.0 %collective-permute-start.9 = (bf16[11,16,512]{2,1,0:T(8,128)(2,1)S(1)}, bf16[11,16,512]{2,1,0:T(8,128)(2,1)S(1)}, u32[]{:S(2)}, u32[]{:S(2)}) collective-permute-start(bf16[11,16,512]{2,1,0:T(8,128)(2,1)S(1)} %bitcast_dynamic-update-slice_fusion), channel_id=1, source_target_pairs={{0,16},{4,20},{8,24},{12,28},{16,0},{20,4},{24,8},{28,12},{1,17},{... | collective-permute-start | bytes 540680 | tf_op jit(solution)/shard_map/ppermute | solution.py:916
  18.9 3.1 %collective-permute-start = (bf16[512,640]{1,0:T(8,128)(2,1)}, bf16[512,640]{1,0:T(8,128)(2,1)}, u32[]{:S(2)}, u32[]{:S(2)}) collective-permute-start(bf16[512,640]{1,0:T(8,128)(2,1)} %get-tuple-element.221), channel_id=1, source_target_pairs={{1,3},{3,1},{5,7},{7,5},{9,11},{11,9},{13,15},{15,13},{17,19},{19,... | collective-permute-start | bytes 1966088 | tf_op jit(solution)/shard_map/ppermute | solution.py:881
  29.7 6.5 %collective-permute-done.5 = bf16[4,16,1536]{2,1,0:T(8,128)(2,1)S(1)} collective-permute-done((bf16[4,16,1536]{2,1,0:T(8,128)(2,1)S(1)}, bf16[4,16,1536]{2,1,0:T(8,128)(2,1)S(1)}, u32[]{:S(2)}, u32[]{:S(2)}) %collective-permute-start.5) | collective-permute-done | bytes 196640 | tf_op jit(solution)/shard_map/ppermute | solution.py:912
  41.4 4.6 %embed.1 = (bf16[1024,512]{1,0:T(8,128)(2,1)S(1)}, bf16[1024,128]{1,0:T(8,128)(2,1)S(1)}, f32[1024,128]{1,0:T(8,128)S(1)}) custom-call(bf16[1024,512]{1,0:T(8,128)(2,1)S(1)} %fusion.2.x_ref.refs_1_, s32[1024,8]{1,0:T(8,128)S(1)} %bitcast.100, bf16[512,256]{1,0:T(8,128)(2,1)S(1)} %bitcast.96), custom_call_target="tpu_custom_call" | custom-call | flops 268435456 | bytes 4194304 | tf_op jit(solution)/shard_map/embed/pallas_call | solution.py:135
  52.4 4.4 %collective-permute-done.11 = bf16[4,6,16,512]{3,2,1,0:T(8,128)(2,1)S(1)} collective-permute-done((bf16[4,6,16,512]{3,2,1,0:T(8,128)(2,1)S(1)}, bf16[4,6,16,512]{3,2,1,0:T(8,128)(2,1)S(1)}, u32[]{:S(2)}, u32[]{:S(2)}) %collective-permute-start.11) | collective-permute-done | bytes 393248 | tf_op jit(solution)/shard_map/ppermute | solution.py:912
  64.4 3.8 %collective-permute-done.18.refs_2_ = bf16[2,512,128]{2,1,0:T(8,128)(2,1)S(1)} collective-permute-done((bf16[2,512,128]{2,1,0:T(8,128)(2,1)}, bf16[2,512,128]{2,1,0:T(8,128)(2,1)S(1)}, u32[]{:S(2)}, u32[]{:S(2)}) %collective-permute-start.18) | collective-permute-done | bytes 262176 | tf_op jit(solution)/shard_map/ppermute | solution.py:908
  73.5 6.1 %query.1 = (bf16[8,1024,128]{2,1,0:T(8,128)(2,1)S(1)}, bf16[512,1536]{1,0:T(8,128)(2,1)S(1)}) custom-call(s32[1]{0:T(128)} %bitcast.me_ref.refs_0_, bf16[1024,512]{1,0:T(8,128)(2,1)S(1)} %copy-done.8, s32[1024,8]{1,0:T(8,128)S(1)} %bitcast.101, bf16[16,16,1536]{2,1,0:T(8,128)(2,1)S(1)} %bitcast.109, bf16[16,16,1536]{2,1,0:T(8,128)(2,1)S(1)} %copy-done.19), custom_call_target="tpu_custom_call" | custom-call | flops 1610612736 | bytes 5767168 | tf_op jit(solution)/shard_map/query/pallas_call | solution.py:183
  84.6 14.4 %attend.1 = (f32[8,1024,128]{2,1,0:T(8,128)S(1)}, f32[1024,128]{1,0:T(8,128)S(1)}, bf16[4096,128]{1,0:T(8,128)(2,1)S(1)}, bf16[4096,128]{1,0:T(8,128)(2,1)S(1)}) custom-call(s32[3,8]{1,0:T(4,128)S(1)} %add_add_fusion.place_ref.refs_0_, bf16[8,1024,128]{2,1,0:T(8,128)(2,1)S(1)} %get-tuple-element.101.q_ref.refs_1_, bf16[2,512,128]{2,1,0:T(8,128)(2,1)S(1)} %bitcast.113, ...), custom_call_target="tpu_custom_call" | custom-call | flops 34359738368 | bytes 8388608 | tf_op jit(solution)/shard_map/attend/pallas_call | solution.py:319
  103.7 6.8 %collective-permute-done.16 = bf16[512,512]{1,0:T(8,128)(2,1)S(1)} collective-permute-done((bf16[512,512]{1,0:T(8,128)(2,1)S(1)}, bf16[512,512]{1,0:T(8,128)(2,1)S(1)}, u32[]{:S(2)}, u32[]{:S(2)}) %collective-permute-start.16) | collective-permute-done | bytes 524320 | tf_op jit(solution)/shard_map/ppermute | solution.py:881
  112.5 38.2 %middle.1 = (bf16[1024,512]{1,0:T(8,128)(2,1)}, f32[1024,512]{1,0:T(8,128)}, bf16[8,1024,128]{2,1,0:T(8,128)(2,1)}, f32[1024,128]{1,0:T(8,128)S(1)}, bf16[1024,1...) custom-call(s32[1]{0:T(128)} %bitcast.me_ref.refs_0_, ...), custom_call_target="tpu_custom_call" | custom-call | flops 17716740096 | bytes 8388608 | tf_op jit(solution)/shard_map/middle/pallas_call | solution.py:762
  161.6 6.2 %attend_back.4 = (bf16[256,1536]{1,0:T(8,128)(2,1)S(1)}, f32[2,64,4096]{2,1,0:T(8,128)S(1)}) custom-call(s32[3,8]{1,0:T(4,128)S(1)} %add_add_fusion.place_ref.refs_0_, bf16[8,1024,128]{2,1,0:T(8,128)(2,1)S(1)} %copy-done.25, bf16[8,1024,128]{2,1,0:T(8,128)(2,1)S(1)} %copy-done.26, f32[1024,128]{1,0:T(8,128)S(1)} %get-tuple-element.103.refs_3_, ...), custom_call_target="tpu_custom_call" | custom-call | flops 10737418240 | bytes 2097152 | tf_op jit(solution)/shard_map/attend_back/pallas_call | solution.py:522
  173.5 17.6 %collective-permute-start.29 = (bf16[2,4,80,512]{3,2,1,0:T(8,128)(2,1)S(1)}, bf16[2,4,80,512]{3,2,1,0:T(8,128)(2,1)S(1)}, u32[]{:S(2)}, u32[]{:S(2)}) collective-permute-start(bf16[2,4,80,512]{3,2,1,0:T(8,128)(2,1)S(1)} %get-tuple-element.132), channel_id=1, source_target_pairs={{0,4},{4,0},{8,12},{12,8},{16,20},{20,16},{24,28},{28,24},{1,5},{5... | collective-permute-start | bytes 1966088 | tf_op jit(solution)/shard_map/ppermute | solution.py:912
  191.1 6.7 %attend_back.5 = (bf16[256,1536]{1,0:T(8,128)(2,1)S(1)}, f32[2,64,4096]{2,1,0:T(8,128)S(1)}) custom-call(s32[3,8]{1,0:T(4,128)S(1)} %add_add_fusion.place_ref.refs_0_, bf16[8,1024,128]{2,1,0:T(8,128)(2,1)S(1)} %copy-done.25, bf16[8,1024,128]{2,1,0:T(8,128)(2,1)S(1)} %copy-done.26, f32[1024,128]{1,0:T(8,128)S(1)} %get-tuple-element.103.refs_3_, ...), custom_call_target="tpu_custom_call" | custom-call | flops 10737418240 | bytes 2097152 | tf_op jit(solution)/shard_map/attend_back/pallas_call | solution.py:522
  197.8 7.3 %collective-permute-done.29 = bf16[2,4,80,512]{3,2,1,0:T(8,128)(2,1)S(1)} collective-permute-done((bf16[2,4,80,512]{3,2,1,0:T(8,128)(2,1)S(1)}, bf16[2,4,80,512]{3,2,1,0:T(8,128)(2,1)S(1)}, u32[]{:S(2)}, u32[]{:S(2)}) %collective-permute-start.29) | collective-permute-done | bytes 655392 | tf_op jit(solution)/shard_map/ppermute | solution.py:912
  209.9 6.9 %attend_back.6 = (bf16[256,1536]{1,0:T(8,128)(2,1)S(1)}, f32[2,64,4096]{2,1,0:T(8,128)S(1)}) custom-call(s32[3,8]{1,0:T(4,128)S(1)} %add_add_fusion.place_ref.refs_0_, bf16[8,1024,128]{2,1,0:T(8,128)(2,1)S(1)} %copy-done.25, bf16[8,1024,128]{2,1,0:T(8,128)(2,1)S(1)} %copy-done.26, f32[1024,128]{1,0:T(8,128)S(1)} %get-tuple-element.103.refs_3_, ...), custom_call_target="tpu_custom_call" | custom-call | flops 10737418240 | bytes 2097152 | tf_op jit(solution)/shard_map/attend_back/pallas_call | solution.py:522
  217.2 7.4 %collective-permute-start.43 = (bf16[176,512]{1,0:T(8,128)(2,1)S(1)}, bf16[176,512]{1,0:T(8,128)(2,1)S(1)}, u32[]{:S(2)}, u32[]{:S(2)}) collective-permute-start(bf16[176,512]{1,0:T(8,128)(2,1)S(1)} %get-tuple-element.232), channel_id=1, source_target_pairs={{0,16},{4,20},{8,24},{12,28},{16,0},{20,4},{24,8},{28,12},{1,17},{... | collective-permute-start | bytes 540680 | tf_op jit(solution)/shard_map/ppermute | solution.py:916
  224.7 8.2 %attend_back.7 = (bf16[256,1536]{1,0:T(8,128)(2,1)S(1)}, bf16[2,2,512,128]{3,2,1,0:T(8,128)(2,1)S(1)}, bf16[2,2,512,128]{3,2,1,0:T(8,128)(2,1)S(1)}, bf16[2,4,2,...) custom-call(s32[3,8]{1,0:T(4,128)S(1)} %add_add_fusion.place_ref.refs_0_, ...), custom_call_target="tpu_custom_call" | custom-call | flops 10737418240 | bytes 2097152 | tf_op jit(solution)/shard_map/attend_back/pallas_call | solution.py:522
  232.9 2.9 collective-permute-start.34
  237.8 11.8 %collective-permute-start.35 = (bf16[4,2,16,1536]{3,2,1,0:T(8,128)(2,1)S(1)}, bf16[4,2,16,1536]{3,2,1,0:T(8,128)(2,1)S(1)}, u32[]{:S(2)}, u32[]{:S(2)}) collective-permute-start(bf16[4,2,16,1536]{3,2,1,0:T(8,128)(2,1)S(1)} %fusion.11), channel_id=1, source_target_pairs={{0,4},{4,0},{8,12},{12,8},{16,20},{20,16},{24,28},{28,24},{1,5},{5... | collective-permute-start | bytes 1179656 | tf_op jit(solution)/shard_map/ppermute | solution.py:912
  252.4 6.4 %collective-permute-done.35 = bf16[4,2,16,1536]{3,2,1,0:T(8,128)(2,1)S(1)} collective-permute-done((bf16[4,2,16,1536]{3,2,1,0:T(8,128)(2,1)S(1)}, bf16[4,2,16,1536]{3,2,1,0:T(8,128)(2,1)S(1)}, u32[]{:S(2)}, u32[]{:S(2)}) %collective-permute-start.35) | collective-permute-done | bytes 393248 | tf_op jit(solution)/shard_map/ppermute | solution.py:912
  263.3 3.9 %finish.1 = (bf16[1024,512]{1,0:T(8,128)(2,1)S(1)}, bf16[512,256]{1,0:T(8,128)(2,1)}) custom-call(bf16[1024,512]{1,0:T(8,128)(2,1)S(1)} %copy-done.1, bf16[1024,512]{1,0:T(8,128)(2,1)S(1)} %copy-done.9, f32[1024,512]{1,0:T(8,128)S(1)} %copy-done.2, f32[1024,512]{1,0:T(8,128)S(1)} %query_back.1.dh_ref, bf16[1024,128]{1,0:T(8,128)(2,1)S(1)} %bitcast.107, ...), custom_call_target="tpu_custom_call" | custom-call | flops 402653184 | bytes 8388608 | tf_op jit(solution)/shard_map/finish/pallas_call | solution.py:844
  267.3 6.0 %all-to-all-start.1 = ((bf16[32,16,256]{2,1,0:T(8,128)(2,1)}), bf16[32,16,256]{2,1,0:T(8,128)(2,1)S(1)}, u32[]{:S(2)}, u32[]{:S(2)}) async-start(bf16[32,16,256]{2,1,0:T(8,128)(2,1)} %bitcast.50), calls=%async_computation.1 | async-start | bytes 524288 | tf_op jit(solution)/shard_map/all_to_all | solution.py:1160
  280.3 3.3 %all-to-all-done.1 = bf16[32,16,256]{2,1,0:T(8,128)(2,1)S(1)} async-done(((bf16[32,16,256]{2,1,0:T(8,128)(2,1)}), bf16[32,16,256]{2,1,0:T(8,128)(2,1)S(1)}, u32[]{:S(2)}, u32[]{:S(2)}) %all-to-all-start.1) | async-done | bytes 262176 | tf_op jit(solution)/shard_map/all_to_all | solution.py:1160
  294.4 3.0 all-to-all-done.2.squares_ref
  (244 shorter events, 107.0 us)
Async XLA Ops:
  15.8 13.7 %collective-permute-start.9 = (bf16[11,16,512]{2,1,0:T(8,128)(2,1)S(1)}, bf16[11,16,512]{2,1,0:T(8,128)(2,1)S(1)}, u32[]{:S(2)}, u32[]{:S(2)}) collective-permute-start(bf16[11,16,512]{2,1,0:T(8,128)(2,1)S(1)} %bitcast_dynamic-update-slice_fusion), channel_id=1, source_target_pairs={{0,16},{4,20},{8,24},{12,28},{16,0},{20,4},{24,8},{28,12},{1,17},{... | collective-permute-start | bytes 540680 | tf_op jit(solution)/shard_map/ppermute | solution.py:916
  18.9 18.3 %collective-permute-start = (bf16[512,640]{1,0:T(8,128)(2,1)}, bf16[512,640]{1,0:T(8,128)(2,1)}, u32[]{:S(2)}, u32[]{:S(2)}) collective-permute-start(bf16[512,640]{1,0:T(8,128)(2,1)} %get-tuple-element.221), channel_id=1, source_target_pairs={{1,3},{3,1},{5,7},{7,5},{9,11},{11,9},{13,15},{15,13},{17,19},{19,... | collective-permute-start | bytes 1966088 | tf_op jit(solution)/shard_map/ppermute | solution.py:881
  22.0 17.3 %collective-permute-start.1 = (bf16[512,640]{1,0:T(8,128)(2,1)}, bf16[512,640]{1,0:T(8,128)(2,1)}, u32[]{:S(2)}, u32[]{:S(2)}) collective-permute-start(bf16[512,640]{1,0:T(8,128)(2,1)} %get-tuple-element.220), channel_id=1, source_target_pairs={{0,1},{1,2},{2,3},{3,0},{4,5},{5,6},{6,7},{7,4},{8,9},{9,10},{10,1... | collective-permute-start | bytes 1966088 | tf_op jit(solution)/shard_map/ppermute | solution.py:880
  25.3 16.1 %all-to-all-start = ((bf16[32,16,256]{2,1,0:T(8,128)(2,1)}), bf16[32,16,256]{2,1,0:T(8,128)(2,1)S(1)}, u32[]{:S(2)}, u32[]{:S(2)}) async-start(bf16[32,16,256]{2,1,0:T(8,128)(2,1)} %broadcast_in_dim.25), calls=%async_computation | async-start | bytes 524288 | tf_op jit(solution)/shard_map/all_to_all | solution.py:1039
  49.9 19.6 %collective-permute-start.7 = (bf16[16,16,1536]{2,1,0:T(8,128)(2,1)S(1)}, bf16[16,16,1536]{2,1,0:T(8,128)(2,1)S(1)}, u32[]{:S(2)}, u32[]{:S(2)}) collective-permute-start(bf16[16,16,1536]{2,1,0:T(8,128)(2,1)S(1)} %bitcast.108), channel_id=1, source_target_pairs={{0,1},{1,0},{2,3},{3,2},{4,5},{5,4},{6,7},{7,6},{8,9},{9,8},{10,11... | collective-permute-start | bytes 2359304 | tf_op jit(solution)/shard_map/ppermute | solution.py:904
  57.8 22.7 %collective-permute-start.13 = (bf16[2,4,6,16,512]{4,3,2,1,0:T(8,128)(2,1)}, bf16[2,4,6,16,512]{4,3,2,1,0:T(8,128)(2,1)}, u32[]{:S(2)}, u32[]{:S(2)}) collective-permute-start(bf16[2,4,6,16,512]{4,3,2,1,0:T(8,128)(2,1)} %pad_maximum_fusion.4.refs_7_), channel_id=1, source_target_pairs={{0,1},{1,0},{2,3},{3,2},{4,5},{5,4},{6,7},{7,6},{8,9},{9,8},{10,11... | collective-permute-start | bytes 2359304 | tf_op jit(solution)/shard_map/ppermute | solution.py:904
  60.5 19.1 %collective-permute-start.14 = (bf16[2,4,5,16,512]{4,3,2,1,0:T(8,128)(2,1)}, bf16[2,4,5,16,512]{4,3,2,1,0:T(8,128)(2,1)}, u32[]{:S(2)}, u32[]{:S(2)}) collective-permute-start(bf16[2,4,5,16,512]{4,3,2,1,0:T(8,128)(2,1)} %pad_maximum_fusion.7.refs_9_), channel_id=1, source_target_pairs={{0,1},{1,0},{2,3},{3,2},{4,5},{5,4},{6,7},{7,6},{8,9},{9,8},{10,11... | collective-permute-start | bytes 1966088 | tf_op jit(solution)/shard_map/ppermute | solution.py:904
  61.7 20.1 %collective-permute-start.17 = (bf16[2,512,128]{2,1,0:T(8,128)(2,1)}, bf16[2,512,128]{2,1,0:T(8,128)(2,1)S(1)}, u32[]{:S(2)}, u32[]{:S(2)}) collective-permute-start(bf16[2,512,128]{2,1,0:T(8,128)(2,1)} %bitcast.112), channel_id=1, source_target_pairs={{0,1},{1,0},{2,3},{3,2},{4,5},{5,4},{6,7},{7,6},{8,9},{9,8},{10,11... | collective-permute-start | bytes 786440 | tf_op jit(solution)/shard_map/ppermute | solution.py:904
  68.2 16.4 %collective-permute-start.19 = (bf16[2,512,128]{2,1,0:T(8,128)(2,1)S(1)}, bf16[2,512,128]{2,1,0:T(8,128)(2,1)S(1)}, u32[]{:S(2)}, u32[]{:S(2)}) collective-permute-start(bf16[2,512,128]{2,1,0:T(8,128)(2,1)S(1)} %collective-permute-done.18.refs_2_), channel_id=1, source_target_pairs={{0,1},{1,0},{2,3},{3,2},{4,5},{5,4},{6,7},{7,6},{8,9},{9,8},{10,11... | collective-permute-start | bytes 786440 | tf_op jit(solution)/shard_map/ppermute | solution.py:904
  70.5 30.6 %collective-permute-start.21 = (bf16[2,4,5,16,512]{4,3,2,1,0:T(8,128)(2,1)}, bf16[2,4,5,16,512]{4,3,2,1,0:T(8,128)(2,1)S(1)}, u32[]{:S(2)}, u32[]{:S(2)}) collective-permute-start(bf16[2,4,5,16,512]{4,3,2,1,0:T(8,128)(2,1)} %pad_maximum_fusion.7.refs_9_), channel_id=1, source_target_pairs={{0,4},{4,0},{8,12},{12,8},{16,20},{20,16},{24,28},{28,24},{1,5},{5... | collective-permute-start | bytes 1966088 | tf_op jit(solution)/shard_map/ppermute | solution.py:912
  79.7 21.4 %collective-permute-start.20 = (bf16[2,4,6,16,512]{4,3,2,1,0:T(8,128)(2,1)}, bf16[2,4,6,16,512]{4,3,2,1,0:T(8,128)(2,1)S(1)}, u32[]{:S(2)}, u32[]{:S(2)}) collective-permute-start(bf16[2,4,6,16,512]{4,3,2,1,0:T(8,128)(2,1)} %pad_maximum_fusion.4.refs_7_), channel_id=1, source_target_pairs={{0,2},{2,0},{1,3},{3,1},{4,6},{6,4},{5,7},{7,5},{8,10},{10,8},{9,1... | collective-permute-start | bytes 2359304 | tf_op jit(solution)/shard_map/ppermute | solution.py:908
  80.6 23.1 %collective-permute-start.15 = (bf16[512,512]{1,0:T(8,128)(2,1)S(1)}, bf16[512,512]{1,0:T(8,128)(2,1)S(1)}, u32[]{:S(2)}, u32[]{:S(2)}) collective-permute-start(bf16[512,512]{1,0:T(8,128)(2,1)S(1)} %get-tuple-element.229), channel_id=1, source_target_pairs={{0,1},{1,2},{2,3},{3,0},{4,5},{5,6},{6,7},{7,4},{8,9},{9,10},{10,1... | collective-permute-start | bytes 1572872 | tf_op jit(solution)/shard_map/ppermute | solution.py:880
  81.8 28.7 %collective-permute-start.16 = (bf16[512,512]{1,0:T(8,128)(2,1)S(1)}, bf16[512,512]{1,0:T(8,128)(2,1)S(1)}, u32[]{:S(2)}, u32[]{:S(2)}) collective-permute-start(bf16[512,512]{1,0:T(8,128)(2,1)S(1)} %get-tuple-element.228), channel_id=1, source_target_pairs={{1,3},{3,1},{5,7},{7,5},{9,11},{11,9},{13,15},{15,13},{17,19},{19,... | collective-permute-start | bytes 1572872 | tf_op jit(solution)/shard_map/ppermute | solution.py:881
  151.6 17.7 %collective-permute-start.26 = (bf16[2,2,4,96,512]{4,3,2,1,0:T(8,128)(2,1)}, bf16[2,2,4,96,512]{4,3,2,1,0:T(8,128)(2,1)}, u32[]{:S(2)}, u32[]{:S(2)}) collective-permute-start(bf16[2,2,4,96,512]{4,3,2,1,0:T(8,128)(2,1)} %get-tuple-element.121), channel_id=1, source_target_pairs={{0,1},{1,0},{2,3},{3,2},{4,5},{5,4},{6,7},{7,6},{8,9},{9,8},{10,11... | collective-permute-start | bytes 4718600 | tf_op jit(solution)/shard_map/ppermute | solution.py:904
  151.6 17.7 %collective-permute-start.27 = (bf16[2,2,4,80,512]{4,3,2,1,0:T(8,128)(2,1)}, bf16[2,2,4,80,512]{4,3,2,1,0:T(8,128)(2,1)S(1)}, u32[]{:S(2)}, u32[]{:S(2)}) collective-permute-start(bf16[2,2,4,80,512]{4,3,2,1,0:T(8,128)(2,1)} %get-tuple-element.122), channel_id=1, source_target_pairs={{0,1},{1,0},{2,3},{3,2},{4,5},{5,4},{6,7},{7,6},{8,9},{9,8},{10,11... | collective-permute-start | bytes 3932168 | tf_op jit(solution)/shard_map/ppermute | solution.py:904
  153.6 14.2 %collective-permute-start.24 = (bf16[512,512]{1,0:T(8,128)(2,1)S(1)}, bf16[512,512]{1,0:T(8,128)(2,1)S(1)}, u32[]{:S(2)}, u32[]{:S(2)}) collective-permute-start(bf16[512,512]{1,0:T(8,128)(2,1)S(1)} %get-tuple-element.227), channel_id=1, source_target_pairs={{1,3},{3,1},{5,7},{7,5},{9,11},{11,9},{13,15},{15,13},{17,19},{19,... | collective-permute-start | bytes 1572872 | tf_op jit(solution)/shard_map/ppermute | solution.py:893
  172.6 32.4 %collective-permute-start.28 = (bf16[2,4,96,512]{3,2,1,0:T(8,128)(2,1)S(1)}, bf16[2,4,96,512]{3,2,1,0:T(8,128)(2,1)S(1)}, u32[]{:S(2)}, u32[]{:S(2)}) collective-permute-start(bf16[2,4,96,512]{3,2,1,0:T(8,128)(2,1)S(1)} %get-tuple-element.131), channel_id=1, source_target_pairs={{0,2},{2,0},{1,3},{3,1},{4,6},{6,4},{5,7},{7,5},{8,10},{10,8},{9,1... | collective-permute-start | bytes 2359304 | tf_op jit(solution)/shard_map/ppermute | solution.py:908
  173.5 31.6 %collective-permute-start.29 = (bf16[2,4,80,512]{3,2,1,0:T(8,128)(2,1)S(1)}, bf16[2,4,80,512]{3,2,1,0:T(8,128)(2,1)S(1)}, u32[]{:S(2)}, u32[]{:S(2)}) collective-permute-start(bf16[2,4,80,512]{3,2,1,0:T(8,128)(2,1)S(1)} %get-tuple-element.132), channel_id=1, source_target_pairs={{0,4},{4,0},{8,12},{12,8},{16,20},{20,16},{24,28},{28,24},{1,5},{5... | collective-permute-start | bytes 1966088 | tf_op jit(solution)/shard_map/ppermute | solution.py:912
  217.2 19.7 %collective-permute-start.42 = (bf16[176,512]{1,0:T(8,128)(2,1)S(1)}, bf16[176,512]{1,0:T(8,128)(2,1)S(1)}, u32[]{:S(2)}, u32[]{:S(2)}) collective-permute-start(bf16[176,512]{1,0:T(8,128)(2,1)S(1)} %get-tuple-element.230), channel_id=1, source_target_pairs={{0,8},{4,12},{8,0},{12,4},{16,24},{20,28},{24,16},{28,20},{1,9},{5... | collective-permute-start | bytes 540680 | tf_op jit(solution)/shard_map/ppermute | solution.py:916
  217.2 19.7 %collective-permute-start.43 = (bf16[176,512]{1,0:T(8,128)(2,1)S(1)}, bf16[176,512]{1,0:T(8,128)(2,1)S(1)}, u32[]{:S(2)}, u32[]{:S(2)}) collective-permute-start(bf16[176,512]{1,0:T(8,128)(2,1)S(1)} %get-tuple-element.232), channel_id=1, source_target_pairs={{0,16},{4,20},{8,24},{12,28},{16,0},{20,4},{24,8},{28,12},{1,17},{... | collective-permute-start | bytes 540680 | tf_op jit(solution)/shard_map/ppermute | solution.py:916
  237.8 21.0 %collective-permute-start.35 = (bf16[4,2,16,1536]{3,2,1,0:T(8,128)(2,1)S(1)}, bf16[4,2,16,1536]{3,2,1,0:T(8,128)(2,1)S(1)}, u32[]{:S(2)}, u32[]{:S(2)}) collective-permute-start(bf16[4,2,16,1536]{3,2,1,0:T(8,128)(2,1)S(1)} %fusion.11), channel_id=1, source_target_pairs={{0,4},{4,0},{8,12},{12,8},{16,20},{20,16},{24,28},{28,24},{1,5},{5... | collective-permute-start | bytes 1179656 | tf_op jit(solution)/shard_map/ppermute | solution.py:912
  267.3 16.3 %all-to-all-start.1 = ((bf16[32,16,256]{2,1,0:T(8,128)(2,1)}), bf16[32,16,256]{2,1,0:T(8,128)(2,1)S(1)}, u32[]{:S(2)}, u32[]{:S(2)}) async-start(bf16[32,16,256]{2,1,0:T(8,128)(2,1)} %bitcast.50), calls=%async_computation.1 | async-start | bytes 524288 | tf_op jit(solution)/shard_map/all_to_all | solution.py:1160
  275.7 16.2 %collective-permute-start.39 = (bf16[512,512]{1,0:T(8,128)(2,1)}, bf16[512,512]{1,0:T(8,128)(2,1)S(1)}, u32[]{:S(2)}, u32[]{:S(2)}) collective-permute-start(bf16[512,512]{1,0:T(8,128)(2,1)} %get-tuple-element.223), channel_id=1, source_target_pairs={{1,3},{3,1},{5,7},{7,5},{9,11},{11,9},{13,15},{15,13},{17,19},{19,... | collective-permute-start | bytes 1572872 | tf_op jit(solution)/shard_map/ppermute | solution.py:893
  277.7 14.9 %collective-permute-start.40 = (bf16[512,512]{1,0:T(8,128)(2,1)S(1)}, bf16[512,512]{1,0:T(8,128)(2,1)S(1)}, u32[]{:S(2)}, u32[]{:S(2)}) collective-permute-start(bf16[512,512]{1,0:T(8,128)(2,1)S(1)} %get-tuple-element.222), channel_id=1, source_target_pairs={{1,0},{2,1},{3,2},{0,3},{5,4},{6,5},{7,6},{4,7},{9,8},{10,9},{11,1... | collective-permute-start | bytes 1572872 | tf_op jit(solution)/shard_map/ppermute | solution.py:892
  (70 other events, 610.6 us)
